TPU v7x, 32 devices: a whole 2x2x4 slice. The times are simulated.
32 devices in a mesh: box: 8 (over z, y), col: 4 (over x, core).
Axes of the slice: x: 2, y: 2, z: 4, core: 2. Of those that a mesh axis runs over, the one named last changes fastest.
Arguments:
- box_points: float32 [16, 3, 512], P('box'), may hold values from 0 to 1
- proxy_directions: float32 [3, 1024], P(None, 'col'), may hold values from -1 to 1, as said below
- point_order: int32 [16, 512], P('box'), may hold values from 0 to 511, each once within a row
- neighbour_boxes: int32 [16, 8], P('box'), may hold values from 0 to 15, as said below
- neighbour_places: int32 [16, 8], P('box'), may hold values from 0 to 25
- pivot_inverse: float32 [16, 2, 256], P('box', None, 'col'), may hold values from -6 to 6
Outputs:
- interpolation: float32 [16, 2, 256, 256], P('box', None, None, 'col')
- skeleton_update: float32 [16, 2, 256, 256], P('box', None, 'col')
Inputs may be any that keep to these rules, and one draw needn't show every extreme that they name: `neighbour_boxes`: box g is held by index g // 2 of the box axis. Every entry names a box of the same index or of the index just before or just after it, cyclically. Of the 16 entries of one index's boxes exactly half name boxes of that same index, never the listing box itself; a box may be listed twice in one row. `proxy_directions`: unit vectors.
All inputs are finite; a program needn't handle non-finite values.
Results may differ from a plain program's by a relative error of at most 0.0038.
Values sent between devices are 32-bit elements; how exact they have to be, the bound alone decides.
A program may use at most 64 MiB of HBM per device.

v0:
```python
import math

import jax
import jax.numpy as jnp
from jax import lax
from jax.sharding import PartitionSpec as P

S = 256


wavenumber = 4.0 * math.pi
softening = 0.05
proxy_radius = 1.5
ridge_share = 0.05
highest = lax.Precision.HIGHEST


def padded(block, sides, width):
    for axis, dim in sides:
        count = lax.axis_size(axis)
        forward = [(i, i + 1) for i in range(count - 1)]
        forward.append((count - 1, 0))
        backward = [(target, source) for source, target in forward]
        low = lax.ppermute(
            lax.slice_in_dim(block, block.shape[dim] - width, None, axis=dim), axis, forward
        )
        high = lax.ppermute(lax.slice_in_dim(block, 0, width, axis=dim), axis, backward)
        block = jnp.concatenate([low, block, high], axis=dim)
    return block


def helmholtz(targets, sources):
    distance_sq = jnp.zeros((targets.shape[1], sources.shape[1]), targets.dtype)
    for axis_id in range(3):
        difference = targets[axis_id][:, None] - sources[axis_id][None, :]
        distance_sq = distance_sq + difference * difference
    radius = jnp.sqrt(distance_sq + softening * softening)
    amplitude = 1.0 / (4.0 * math.pi * radius)
    return (amplitude * jnp.cos(wavenumber * radius), amplitude * jnp.sin(wavenumber * radius))


def decode(place_codes):
    full_code = place_codes + (place_codes >= 13).astype(jnp.int32)
    return jnp.stack(
        [full_code // 9 - 1, full_code // 3 % 3 - 1, full_code % 3 - 1], axis=-1
    ).astype(jnp.float32)


def cross_products(real_tile, imag_tile, skel_count):
    stacked = jnp.concatenate([real_tile, imag_tile], axis=0)
    flipped = jnp.concatenate([imag_tile, -real_tile], axis=0)
    left_cols = stacked[:, :skel_count]
    contract = (((0,), (0,)), ((), ()))
    real_cross = lax.dot_general(left_cols, stacked, contract, preferred_element_type=jnp.float32)
    imag_cross = lax.dot_general(left_cols, flipped, contract, preferred_element_type=jnp.float32)
    return jnp.stack([real_cross, imag_cross])


def factor(gram_block):
    real_gram = gram_block[0]
    imag_gram = gram_block[1]
    skel_count = real_gram.shape[0]
    ridge_value = ridge_share * jnp.trace(real_gram) / skel_count
    real_gram = real_gram + ridge_value * jnp.eye(skel_count, dtype=real_gram.dtype)
    upper_half = jnp.concatenate([real_gram, -imag_gram], axis=1)
    lower_half = jnp.concatenate([imag_gram, real_gram], axis=1)
    return jnp.linalg.cholesky(jnp.concatenate([upper_half, lower_half], axis=0))


def apply_inverse(cholesky_factor, right_side):
    stacked = right_side.reshape(2 * right_side.shape[1], right_side.shape[2])
    forward = lax.linalg.triangular_solve(cholesky_factor, stacked, left_side=True, lower=True)
    backward = lax.linalg.triangular_solve(
        cholesky_factor, forward, left_side=True, lower=True, transpose_a=True
    )
    return backward.reshape(right_side.shape)


def pair_update(near_points, own_columns, coefficients, pivot_row):
    skel_count = coefficients.shape[1]
    real_kernel, imag_kernel = helmholtz(near_points, own_columns)
    real_skel = real_kernel[:, :skel_count]
    imag_skel = imag_kernel[:, :skel_count]
    real_rest = real_kernel[:, skel_count:]
    imag_rest = imag_kernel[:, skel_count:]
    matmul_dims = (((1,), (0,)), ((), ()))
    outer_dims = (((1,), (1,)), ((), ()))

    def product(left_side, right_side):
        return lax.dot_general(
            left_side,
            right_side,
            matmul_dims,
            precision=highest,
            preferred_element_type=jnp.float32,
        )

    def outer_product(left_side, right_side):
        return lax.dot_general(
            left_side, right_side, outer_dims, precision=highest, preferred_element_type=jnp.float32
        )

    real_block = real_rest - (
        product(real_skel, coefficients[0]) - product(imag_skel, coefficients[1])
    )
    imag_block = imag_rest - (
        product(real_skel, coefficients[1]) + product(imag_skel, coefficients[0])
    )
    real_weighted = real_block * pivot_row[0][None, :] - imag_block * pivot_row[1][None, :]
    imag_weighted = real_block * pivot_row[1][None, :] + imag_block * pivot_row[0][None, :]
    real_update = outer_product(real_weighted, real_block) - outer_product(
        imag_weighted, imag_block
    )
    imag_update = outer_product(real_weighted, imag_block) + outer_product(
        imag_weighted, real_block
    )
    return -jnp.stack([real_update, imag_update])


def on_device(
    box_points, proxy_directions, point_order, neighbour_boxes, neighbour_places, pivot_inverse
):
    box_count = box_points.shape[0]
    point_count = box_points.shape[2]
    skel_count = S
    rest_width = pivot_inverse.shape[2]
    col_count = lax.axis_size("col")
    col_index = lax.axis_index("col")
    box_index = lax.axis_index("box")
    box_total = lax.axis_size("box")
    ordered = jnp.take_along_axis(
        box_points, jnp.broadcast_to(point_order[:, None, :], box_points.shape), axis=2
    )
    extended = padded(ordered, (("box", 0),), box_count)
    owner_device = neighbour_boxes // box_count
    device_step = jnp.mod(owner_device - box_index + 1, box_total) - 1
    local_slot = (device_step + 1) * box_count + neighbour_boxes % box_count
    shift_table = decode(neighbour_places)
    proxies = 0.5 + proxy_radius * proxy_directions
    group_size = neighbour_boxes.shape[1] // col_count

    def cross_one(which_box):
        own_points = ordered[which_box]
        slot_rows = lax.dynamic_slice_in_dim(
            local_slot[which_box], col_index * group_size, group_size, 0
        )
        shift_rows = lax.dynamic_slice_in_dim(
            shift_table[which_box], col_index * group_size, group_size, 0
        )
        near_points = extended[slot_rows] + shift_rows[:, :, None]
        near_points = jnp.transpose(near_points, (1, 0, 2)).reshape(3, group_size * point_count)
        targets = jnp.concatenate([proxies, near_points], axis=1)
        real_tile, imag_tile = helmholtz(targets, own_points)
        return cross_products(
            real_tile.astype(jnp.bfloat16), imag_tile.astype(jnp.bfloat16), skel_count
        )

    cross_terms = lax.map(cross_one, jnp.arange(box_count, dtype=jnp.int32))
    gram_total = lax.psum(cross_terms[:, :, :, :skel_count], "col")
    rest_terms = lax.psum_scatter(
        cross_terms[:, :, :, skel_count:], "col", scatter_dimension=3, tiled=True
    )
    factors = jax.vmap(factor)(gram_total)
    interpolation = jax.vmap(apply_inverse)(factors, rest_terms)
    own_start = skel_count + col_index * rest_width
    slot_range = jnp.arange(3 * box_count, dtype=jnp.int32)

    def schur_box(which_box, buffer):
        own_points = ordered[which_box]
        own_columns = jnp.concatenate(
            [
                own_points[:, :skel_count],
                lax.dynamic_slice_in_dim(own_points, own_start, rest_width, 1),
            ],
            axis=1,
        )
        near_points = (
            extended[local_slot[which_box]][:, :, :skel_count] + shift_table[which_box][:, :, None]
        )
        coefficients = interpolation[which_box]
        pivot_row = pivot_inverse[which_box]
        updates = jax.vmap(
            lambda points_one: pair_update(points_one, own_columns, coefficients, pivot_row)
        )(near_points)
        one_hot = (local_slot[which_box][:, None] == slot_range[None, :]).astype(jnp.float32)
        return buffer + jnp.einsum("ks,kcij->scij", one_hot, updates, precision=highest)

    buffer = lax.fori_loop(
        0, box_count, schur_box, jnp.zeros((3 * box_count, 2, skel_count, skel_count), jnp.float32)
    )
    reduced = lax.psum_scatter(buffer, "col", scatter_dimension=2, tiled=True)
    outgoing = jnp.concatenate([reduced[:box_count], reduced[2 * box_count :]], axis=0)
    arrived = padded(outgoing, (("box", 0),), box_count)
    skeleton_update = (
        reduced[box_count : 2 * box_count] + arrived[:box_count] + arrived[3 * box_count :]
    )
    return (interpolation, skeleton_update)


def solution(mesh):
    placed = (
        P("box", None, None),
        P(None, "col"),
        P("box", None),
        P("box", None),
        P("box", None),
        P("box", None, "col"),
    )
    return jax.shard_map(
        on_device,
        mesh=mesh,
        in_specs=placed,
        out_specs=(P("box", None, None, "col"), P("box", None, "col", None)),
        check_vma=False,
    )
```

profile of v0, /device:TPU:0, one launch (start us, length us, event | category | flops | bytes accessed | tf_op | source)
XLA Modules:
  0.0 605.4 jit_solution(18040815896717883606)
XLA Ops:
  9.4 30.1 %gather_fusion.2 = f32[3072]{0:T(1024)S(1)} fusion(f32[2,3,512]{2,0,1:T(2,128)S(1)} %copy-done, s32[3072]{0:T(1024)S(1)} %reshape.250), kind=kCustom, calls=%fused_computation.2 | custom fusion | bytes 61440 | tf_op jit(solution)/shard_map/jit(take_along_axis)/gather | solution.py:131
  39.5 6.1 %collective-permute-start.1 = (f32[2,3,512]{2,1,0:T(4,128)S(1)}, f32[2,3,512]{2,1,0:T(4,128)S(1)}, u32[]{:S(2)}, u32[]{:S(2)}) collective-permute-start(f32[2,3,512]{2,1,0:T(4,128)S(1)} %fusion.118), channel_id=1, source_target_pairs={{4,0},{8,4},{12,8},{16,12},{20,16},{24,20},{28,24},{0,28},{5,1},{9... | collective-permute-start | bytes 36872 | tf_op jit(solution)/shard_map/ppermute | solution.py:27
  47.0 5.0 collective-permute-done
  52.0 58.4 %while.31 = (s32[]{:T(128)}, f32[2,2,256,512]{3,2,1,0:T(8,128)S(1)}, s32[2]{0:T(128)S(1)}, s32[2,8]{1,0:T(2,128)S(1)}, s32[]{:T(128)}, /*index=5*/f32[6,3,512]{2...) while((s32[]{:T(128)}, ...), condition=%wide.region_1.2_spmd, body=%wide.region_0.0_spmd.sunk | while | flops 1378492160 | bytes 13771115 | solution.py:158
  55.1 11.7 %fusion.183 = bf16[1280,512]{1,0:T(8,128)(2,1)S(1)} fusion(f32[512]{0:T(512)S(1)} %bitcast.240, f32[1280]{0:T(1024)S(1)} %get-tuple-element.827, f32[512]{0:T(512)S(1)} %bitcast.238, f32[1280]{0:T(1024)S(1)} %get-tuple-element.829, f32[512]{0:T(512)S(1)} %bitcast.236, f32[1280]{0:T(1024)S(1)} %get-tuple-element.831), kind=kLoop, calls=%fused_computation.40.clone.1 | loop fusion | flops 10485760 | bytes 1332224 | tf_op jit(solution)/shard_map/while/body/eval_jaxpr/neg | solution.py:51
  66.8 12.6 %multiply_convert_fusion.3 = (bf16[1280,512]{1,0:T(8,128)(2,1)S(1)}, bf16[1280,512]{1,0:T(8,128)(2,1)S(1)}) fusion(f32[512]{0:T(512)S(1)} %bitcast.241, f32[1280]{0:T(1024)S(1)} %get-tuple-element.827, f32[512]{0:T(512)S(1)} %bitcast.239, f32[1280]{0:T(1024)S(1)} %get-tuple-element.829, f32[512]{0:T(512)S(1)} %bitcast.237, ...), kind=kLoop, calls=%fused_computation.15.clone.2 | loop fusion | flops 9830400 | bytes 2642944 | tf_op jit(solution)/shard_map/while/body/eval_jaxpr/convert_element_type | solution.py:155
  84.3 11.7 %fusion.183 = bf16[1280,512]{1,0:T(8,128)(2,1)S(1)} fusion(f32[512]{0:T(512)S(1)} %bitcast.240, f32[1280]{0:T(1024)S(1)} %get-tuple-element.827, f32[512]{0:T(512)S(1)} %bitcast.238, f32[1280]{0:T(1024)S(1)} %get-tuple-element.829, f32[512]{0:T(512)S(1)} %bitcast.236, f32[1280]{0:T(1024)S(1)} %get-tuple-element.831), kind=kLoop, calls=%fused_computation.40.clone.1 | loop fusion | flops 10485760 | bytes 1332224 | tf_op jit(solution)/shard_map/while/body/eval_jaxpr/neg | solution.py:51
  96.0 12.6 %multiply_convert_fusion.3 = (bf16[1280,512]{1,0:T(8,128)(2,1)S(1)}, bf16[1280,512]{1,0:T(8,128)(2,1)S(1)}) fusion(f32[512]{0:T(512)S(1)} %bitcast.241, f32[1280]{0:T(1024)S(1)} %get-tuple-element.827, f32[512]{0:T(512)S(1)} %bitcast.239, f32[1280]{0:T(1024)S(1)} %get-tuple-element.829, f32[512]{0:T(512)S(1)} %bitcast.237, ...), kind=kLoop, calls=%fused_computation.15.clone.2 | loop fusion | flops 9830400 | bytes 2642944 | tf_op jit(solution)/shard_map/while/body/eval_jaxpr/convert_element_type | solution.py:155
  110.4 1.9 copy.163
  112.3 2.4 copy.172
  114.7 2.5 slice.434
  120.1 47.3 %all-reduce.5.cloned.1.call-done = (f32[2,2,256,256]{2,3,0,1:T(8,128)}, f32[2,2,256,256]{2,1,0,3:T(2,128)}) async-done(((f32[2,2,256,256]{2,3,0,1:T(8,128)}, f32[2,2,256,256]{2,1,0,3:T(2,128)}), (f32[2,2,256,256]{2,3,0,1:T(8,128)}, f32[2,2,256,256]{2,1,0,3:T(2,128)})) %all-reduce.5.cloned.1.call-update) | async-done | bytes 2097168 | tf_op jit(solution)/shard_map/psum | solution.py:159
  167.4 1.9 slice_bitcast_fusion.2
  174.1 2.1 copy.164
  176.2 2.1 fusion.72
  179.6 23.5 %custom-call.36 = f32[2,128,128]{2,1,0:T(8,128)S(1)} custom-call(f32[2,128,128]{2,1,0:T(8,128)S(1)} %cholesky.274), custom_call_target="Cholesky" | custom-call | tf_op jit(solution)/shard_map/vmap(jit(cholesky))/cholesky | solution.py:67
  203.1 19.7 %custom-call.37 = f32[2,1,128,128]{2,3,1,0:T(8,128)S(1)} custom-call(f32[2,1,128,128]{3,2,1,0:T(8,128)S(1)} %select_bitcast_fusion.2), custom_call_target="InvertDiagBlocksLowerTriangular" | custom-call | tf_op jit(solution)/shard_map/vmap(jit(cholesky))/cholesky | solution.py:67
  223.1 1.5 constant_dynamic-update-slice_fusion.3
  224.6 1.5 convolution_subtract_fusion
  226.1 23.5 %custom-call.38 = f32[2,128,128]{2,1,0:T(8,128)S(1)} custom-call(f32[2,128,128]{2,1,0:T(8,128)S(1)} %cholesky.278), custom_call_target="Cholesky" | custom-call | tf_op jit(solution)/shard_map/vmap(jit(cholesky))/cholesky | solution.py:67
  249.6 20.1 %custom-call.39 = f32[2,1,128,128]{2,3,1,0:T(8,128)S(1)} custom-call(f32[2,1,128,128]{3,2,1,0:T(8,128)S(1)} %get-tuple-element.671), custom_call_target="InvertDiagBlocksLowerTriangular" | custom-call | tf_op jit(solution)/shard_map/vmap(jit(cholesky))/cholesky | solution.py:67
  270.1 1.6 convolution_subtract_fusion.1
  271.6 23.5 %custom-call.40 = f32[2,128,128]{2,1,0:T(8,128)S(1)} custom-call(f32[2,128,128]{2,1,0:T(8,128)S(1)} %cholesky.283), custom_call_target="Cholesky" | custom-call | tf_op jit(solution)/shard_map/vmap(jit(cholesky))/cholesky | solution.py:67
  295.1 19.7 %custom-call.41 = f32[2,1,128,128]{2,3,1,0:T(8,128)S(1)} custom-call(f32[2,1,128,128]{3,2,1,0:T(8,128)S(1)} %get-tuple-element.669), custom_call_target="InvertDiagBlocksLowerTriangular" | custom-call | tf_op jit(solution)/shard_map/vmap(jit(cholesky))/cholesky | solution.py:67
  315.1 1.5 convolution_subtract_fusion.2
  316.6 23.7 %custom-call.42 = f32[2,128,128]{2,1,0:T(8,128)S(1)} custom-call(f32[2,128,128]{2,1,0:T(8,128)S(1)} %convolution_subtract_fusion.2), custom_call_target="Cholesky" | custom-call | tf_op jit(solution)/shard_map/vmap(jit(cholesky))/cholesky | solution.py:67
  340.7 1.7 select_select_fusion
  342.4 14.9 %while.32 = (s32[]{:T(128)}, f32[2,512,512]{2,1,0:T(8,128)}, s32[4,2]{0,1:T(2,128)S(1)}, f32[4,2,128,128]{3,2,0,1:T(8,128)}, s32[]{:T(128)}) while((s32[]{:T(128)}, f32[2,512,512]{2,1,0:T(8,128)}, s32[4,2]{0,1:T(2,128)S(1)}, f32[4,2,128,128]{3,2,0,1:T(8,128)}, s32[]{:T(128)}) %tuple.147), condition=%wide.while_cond, body=%wide.while_body.sunk | while | flops 2 | bytes 263277 | solution.py:73
  343.1 3.1 bitcast_dynamic-update-slice_fusion.2
  346.8 3.0 bitcast_dynamic-update-slice_fusion.2
  350.5 3.1 bitcast_dynamic-update-slice_fusion.2
  354.3 3.0 bitcast_dynamic-update-slice_fusion.2
  357.3 79.4 %custom-call.43 = f32[2,4,128,128]{2,3,1,0:T(8,128)S(1)} custom-call(f32[2,4,128,128]{3,2,1,0:T(8,128)} %bitcast.242), custom_call_target="InvertDiagBlocksLowerTriangular" | custom-call | tf_op jit(solution)/shard_map/vmap()/triangular_solve | solution.py:73
  440.2 1.6 convolution_subtract_fusion.8
  447.5 90.3 %while.33 = (s32[]{:T(128)}, f32[6,2,256,256]{3,0,2,1:T(8,128)}, s32[2,8]{1,0:T(2,128)S(1)}, f32[6,3,512]{2,1,0:T(4,128)S(1)}, f32[2,8,3]{1,0,2:T(2,128)S(1)}, /...) while((s32[]{:T(128)}, f32[6,2,256,256]{3,0,2,1:T(8,128)}, ...), condition=%wide.region_14.15_spmd.clone, body=%wide.region_13.14_spmd.clone.sunk | while | flops 3312066560 | bytes 79216528 | solution.py:188
  469.1 10.8 %cosine_multiply_fusion.2 = (f32[8,256,320]{1,2,0:T(8,128)S(1)}, f32[8,256,320]{1,2,0:T(8,128)S(1)}) fusion(f32[320]{0:T(512)S(1)} %get-tuple-element.849, f32[8,256]{1,0:T(8,128)S(1)} %get-tuple-element.852, f32[320]{0:T(512)S(1)} %get-tuple-element.853, f32[8,256]{1,0:T(8,128)S(1)} %get-tuple-element.854, f32[320]{0:T(512)S(1)} %get-tuple-element.855, ...), kind=kLoop, calls=%fused_computation.47.clone.1 | loop fusion | flops 8519680 | bytes 5271296 | tf_op jit(solution)/shard_map/while/body/eval_jaxpr/vmap()/mul | solution.py:39
  479.8 1.5 fusion.202
  481.3 1.5 fusion.203
  484.3 1.5 fusion.201
  485.8 1.9 fusion.205
  487.8 2.0 subtract_bitcast_fusion.2
  489.8 1.9 fusion.204
  491.7 2.0 add_bitcast_fusion.3
  494.1 1.8 copy-done.1
  495.9 5.0 select_add_fusion.2
  501.0 1.9 copy-done.2
  503.9 10.8 %cosine_multiply_fusion.2 = (f32[8,256,320]{1,2,0:T(8,128)S(1)}, f32[8,256,320]{1,2,0:T(8,128)S(1)}) fusion(f32[320]{0:T(512)S(1)} %get-tuple-element.849, f32[8,256]{1,0:T(8,128)S(1)} %get-tuple-element.852, f32[320]{0:T(512)S(1)} %get-tuple-element.853, f32[8,256]{1,0:T(8,128)S(1)} %get-tuple-element.854, f32[320]{0:T(512)S(1)} %get-tuple-element.855, ...), kind=kLoop, calls=%fused_computation.47.clone.1 | loop fusion | flops 8519680 | bytes 5271296 | tf_op jit(solution)/shard_map/while/body/eval_jaxpr/vmap()/mul | solution.py:39
  514.7 1.5 fusion.202
  516.2 1.5 fusion.203
  519.2 1.5 fusion.201
  520.7 1.9 fusion.205
  522.6 2.0 subtract_bitcast_fusion.2
  524.6 1.9 fusion.204
  526.6 2.0 add_bitcast_fusion.3
  529.0 1.8 copy-done.1
  530.8 5.0 select_add_fusion.2
  535.8 1.9 copy-done.2
  537.8 5.0 copy.184
  542.8 38.0 %reduce-scatter.2.cloned.1.call-done = f32[6,2,64,256]{3,2,1,0:T(8,128)} async-done(((f32[6,2,256,256]{3,2,1,0:T(8,128)}), f32[6,2,64,256]{3,2,1,0:T(8,128)}) %reduce-scatter.2.cloned.1.call-update) | async-done | bytes 786448 | tf_op jit(solution)/shard_map/reduce_scatter | solution.py:191
  581.8 1.5 collective-permute-start.2
  583.3 3.2 collective-permute-start.3
  586.6 7.8 %collective-permute-done.2 = f32[2,2,64,256]{3,2,1,0:T(8,128)S(1)} collective-permute-done((f32[2,2,64,256]{3,2,1,0:T(8,128)S(1)}, f32[2,2,64,256]{3,2,1,0:T(8,128)S(1)}, u32[]{:S(2)}, u32[]{:S(2)}) %collective-permute-start.2) | collective-permute-done | bytes 262176 | tf_op jit(solution)/shard_map/ppermute | solution.py:24
  594.3 2.2 collective-permute-done.3
  596.5 1.7 fusion.79
  (169 shorter events, 37.8 us)
Async XLA Ops:
  7.2 2.2 copy-start
  7.2 160.2 %all-reduce.5.cloned.1.call-start = ((), (), s32[]{:S(2)}) async-start(), calls=%async_computation.2 | async-start | bytes 4194304 | tf_op jit(solution)/shard_map/psum | solution.py:159
  9.3 30.1 %copy-start.11 = (s32[2,512]{1,0:T(2,128)S(1)}, s32[2,512]{1,0:T(2,128)}, u32[]{:S(2)}) copy-start(s32[2,512]{1,0:T(2,128)} %param.12) | copy-start | bytes 12292
  9.4 36.2 %copy-start.15 = (s32[2,8]{1,0:T(2,128)S(1)}, s32[2,8]{1,0:T(2,128)}, u32[]{:S(2)}) copy-start(s32[2,8]{1,0:T(2,128)} %param.14) | copy-start | bytes 196
  9.4 36.3 %copy-start.13 = (f32[3,256]{1,0:T(4,128)S(1)}, f32[3,256]{1,0:T(4,128)}, u32[]{:S(2)}) copy-start(f32[3,256]{1,0:T(4,128)} %param.11) | copy-start | bytes 9220
  9.4 36.3 %copy-start.14 = (s32[2,8]{1,0:T(2,128)S(1)}, s32[2,8]{1,0:T(2,128)}, u32[]{:S(2)}) copy-start(s32[2,8]{1,0:T(2,128)} %param.13) | copy-start | bytes 196
  39.5 7.5 %collective-permute-start.1 = (f32[2,3,512]{2,1,0:T(4,128)S(1)}, f32[2,3,512]{2,1,0:T(4,128)S(1)}, u32[]{:S(2)}, u32[]{:S(2)}) collective-permute-start(f32[2,3,512]{2,1,0:T(4,128)S(1)} %fusion.118), channel_id=1, source_target_pairs={{4,0},{8,4},{12,8},{16,12},{20,16},{24,20},{28,24},{0,28},{5,1},{9... | collective-permute-start | bytes 36872 | tf_op jit(solution)/shard_map/ppermute | solution.py:27
  45.6 6.4 %collective-permute-start = (f32[2,3,512]{2,1,0:T(4,128)S(1)}, f32[2,3,512]{2,1,0:T(4,128)S(1)}, u32[]{:S(2)}, u32[]{:S(2)}) collective-permute-start(f32[2,3,512]{2,1,0:T(4,128)S(1)} %fusion.118), channel_id=1, source_target_pairs={{0,4},{4,8},{8,12},{12,16},{16,20},{20,24},{24,28},{28,0},{1,5},{5... | collective-permute-start | bytes 36872 | tf_op jit(solution)/shard_map/ppermute | solution.py:24
  114.7 2.5 copy-start.5
  117.2 1.5 copy-start.16
  118.6 462.1 %reduce-scatter.2.cloned.1.call-start = ((), (), s32[]{:S(2)}) async-start(), calls=%async_computation.1 | async-start | bytes 3932160 | tf_op jit(solution)/shard_map/reduce_scatter | solution.py:191
  167.4 5.2 copy-start.6
  178.3 1.3 copy-start.4
  340.6 96.1 %copy-start.8 = (f32[2,128,64]{1,0,2:T(2,128)S(1)}, f32[2,128,64]{1,0,2:T(2,128)}, u32[]{:S(2)}) copy-start(f32[2,128,64]{1,0,2:T(2,128)} %get-tuple-element.667) | copy-start | bytes 196612
  340.7 96.3 %copy-start.7 = (f32[2,128,64]{1,0,2:T(2,128)S(1)}, f32[2,128,64]{1,0,2:T(2,128)}, u32[]{:S(2)}) copy-start(f32[2,128,64]{1,0,2:T(2,128)} %get-tuple-element.666) | copy-start | bytes 196612
  342.4 96.2 %copy-start.10 = (f32[2,128,64]{1,0,2:T(2,128)S(1)}, f32[2,128,64]{1,0,2:T(2,128)}, u32[]{:S(2)}) copy-start(f32[2,128,64]{1,0,2:T(2,128)} %get-tuple-element.665) | copy-start | bytes 196612
  342.4 97.8 %copy-start.9 = (f32[2,128,64]{1,0,2:T(2,128)S(1)}, f32[2,128,64]{1,0,2:T(2,128)}, u32[]{:S(2)}) copy-start(f32[2,128,64]{1,0,2:T(2,128)} %get-tuple-element.664) | copy-start | bytes 196612
  441.8 5.6 copy-start.12
  493.8 2.2 copy-start.1
  501.0 1.9 copy-start.2
  528.6 2.2 copy-start.1
  535.8 1.9 copy-start.2
  537.8 5.0 copy-start.3
  581.8 12.5 %collective-permute-start.2 = (f32[2,2,64,256]{3,2,1,0:T(8,128)S(1)}, f32[2,2,64,256]{3,2,1,0:T(8,128)S(1)}, u32[]{:S(2)}, u32[]{:S(2)}) collective-permute-start(f32[2,2,64,256]{3,2,1,0:T(8,128)S(1)} %get-tuple-element.662), channel_id=1, source_target_pairs={{0,4},{4,8},{8,12},{12,16},{16,20},{20,24},{24,28},{28,0},{1,5},{5... | collective-permute-start | bytes 786440 | tf_op jit(solution)/shard_map/ppermute | solution.py:24
  583.3 13.2 %collective-permute-start.3 = (f32[2,2,64,256]{3,2,1,0:T(8,128)S(1)}, f32[2,2,64,256]{3,2,1,0:T(8,128)S(1)}, u32[]{:S(2)}, u32[]{:S(2)}) collective-permute-start(f32[2,2,64,256]{3,2,1,0:T(8,128)S(1)} %get-tuple-element.663), channel_id=1, source_target_pairs={{4,0},{8,4},{12,8},{16,12},{20,16},{24,20},{28,24},{0,28},{5,1},{9... | collective-permute-start | bytes 786440 | tf_op jit(solution)/shard_map/ppermute | solution.py:27
Sparse Core Ops, SparseCore 0:
  118.7 48.6 all-reduce.4
  542.9 37.7 reduce-scatter.1
where the time goes:
time: 613 us; the launch traced here: 605 us
  other arithmetic  315 us (51%)
  waiting for transfers between devices  101 us (16%)
  local copies, waits for them, and re-layouts  79.1 us (13%)
  matrix products  58.5 us (10%)
  loops' own time  24.4 us (4%)
  between operations  15.7 us (3%)
  starting transfers between devices  10.9 us (2%)
    another operation x16, other arithmetic, factor(): jnp.linalg.cholesky(jnp.concatenate([upper_half, lower_half], axis=0))  154 us
    another operation x5, other arithmetic, apply_inverse(): lax.linalg.triangular_solve(cholesky_factor, forward, left_side=True, low...  81.2 us
    psum x1, waiting for transfers between devices, on_device(): gram_total = lax.psum(cross_terms[:, :, :, :skel_count], 'col')  47.3 us
    reduce_scatter x1, waiting for transfers between devices, on_device(): reduced = lax.psum_scatter(buffer, 'col', scatter_dimension=2, tiled=True)  38 us
    gather x3, local copies, waits for them, and re-layouts, on_device(): jnp.take_along_axis(box_points, jnp.broadcast_to(point_order[:, None, :],...  30.1 us
    convert_element_type x2, other arithmetic, cross_one(): real_tile.astype(jnp.bfloat16)  25.2 us
    neg x2, other arithmetic, cross_products(): flipped = jnp.concatenate([imag_tile, -real_tile], axis=0)  23.3 us
    mul x2, other arithmetic, helmholtz(): amplitude * jnp.cos(wavenumber * radius)  21.5 us
  transfers between devices with their start and end apart: 6, of which 6 were waited for; matrix products, arithmetic and copies ran while one was open for 0% of the time, Pallas kernels for 0%

commit v1 on v0

v1 whole, which is shorter than its diff:
```python
import functools
import math

import jax
import jax.numpy as jnp
from jax import lax
from jax.experimental import pallas as pl
from jax.experimental.pallas import tpu as pltpu
from jax.sharding import PartitionSpec as P

S = 256

softening = 0.05
proxy_radius = 1.5
ridge_share = 0.05
highest = lax.Precision.HIGHEST
NBLK = 32
ROWS = 32

COS = (1.0, -19.73920440673828, 64.93911743164062, -85.45014190673828, 60.16762924194336,
       -25.967599868774414, 6.528658390045166)
SIN = (6.2831854820251465, -41.34170150756836, 81.60513305664062, -76.70301818847656,
       42.02592849731445, -14.899847030639648, 3.2381374835968018)

VMEM = pl.BlockSpec(memory_space=pltpu.VMEM)
SMEM = pl.BlockSpec(memory_space=pltpu.SMEM)


def params(**more):
    return pltpu.CompilerParams(vmem_limit_bytes=48 * 1024 * 1024, **more)


def horner(coefficients, z):
    total = jnp.full_like(z, coefficients[-1])
    for one in coefficients[-2::-1]:
        total = total * z + one
    return total


def kernel_values(tx, ty, tz, sx, sy, sz):
    dx = tx - sx
    dy = ty - sy
    dz = tz - sz
    square = dx * dx + dy * dy + dz * dz + softening * softening
    inverse = lax.rsqrt(square)
    inverse = inverse * (1.5 - 0.5 * square * inverse * inverse)
    turns = 2.0 * (square * inverse)
    part = turns - jnp.floor(turns + 0.5)
    z = part * part
    amplitude = inverse * (1.0 / (4.0 * math.pi))
    return amplitude * horner(COS, z), (amplitude * part) * horner(SIN, z)


def slot_of(nb_ref, where_ref, row, entry, box_count, box_total):
    owner_box = nb_ref[row, entry]
    step = owner_box // box_count - where_ref[0] + 1
    step = jnp.where(step < 0, step + box_total, step)
    step = jnp.where(step >= box_total, step - box_total, step)
    return step * box_count + owner_box % box_count


def dot_tn(a, b):
    return lax.dot_general(a, b, (((0,), (0,)), ((), ())), preferred_element_type=jnp.float32)


def tile_kernel(box_count, box_total, entries, where_ref, nb_ref, place_ref, points_ref, order_ref,
                proxy_ref, cross_ref, kern_ref, tcol, srow, tre, tim):
    count = points_ref.shape[2]
    proxies = proxy_ref.shape[1]
    box = where_ref[1]
    first = where_ref[2] * entries

    def ordered(slot):
        one_hot = (
            lax.broadcasted_iota(jnp.int32, (count, count), 0) == order_ref[slot, 0:1, :]
        ).astype(jnp.float32)
        return lax.dot_general(
            points_ref[slot], one_hot, (((1,), (0,)), ((), ())), precision=highest,
            preferred_element_type=jnp.float32,
        )

    axis_row = lax.broadcasted_iota(jnp.int32, (8, count), 0)
    srow[...] = ordered(box_count + box)
    tcol[0:proxies, 0:8] = jnp.transpose(0.5 + proxy_radius * proxy_ref[...])
    for k in range(entries):
        slot = slot_of(nb_ref, where_ref, box, first + k, box_count, box_total)
        code = place_ref[box, first + k]
        code = jnp.where(code >= 13, code + 1, code)
        shift = [(code // 9 - 1), (code // 3) % 3 - 1, code % 3 - 1]
        move = jnp.where(
            axis_row == 0,
            shift[0].astype(jnp.float32),
            jnp.where(axis_row == 1, shift[1].astype(jnp.float32), shift[2].astype(jnp.float32)),
        )
        start = proxies + k * count
        tcol[start:start + count, 0:8] = jnp.transpose(ordered(slot) + move)

    def strip(start):
        return kernel_values(
            tcol[pl.ds(start, ROWS), 0:1], tcol[pl.ds(start, ROWS), 1:2],
            tcol[pl.ds(start, ROWS), 2:3], srow[0:1, :], srow[1:2, :], srow[2:3, :],
        )

    def store(start, real, imag):
        tre[pl.ds(start, ROWS), :] = real.astype(jnp.bfloat16)
        tim[pl.ds(start, ROWS), :] = imag.astype(jnp.bfloat16)

    def plain(base, rows):
        @pl.loop(0, rows // ROWS)
        def _(i):
            start = pl.multiple_of(base + i * ROWS, ROWS)
            real, imag = strip(start)
            store(start, real, imag)

    def kept(base, k):
        @pl.loop(0, S // ROWS)
        def _(i):
            inner = pl.multiple_of(i * ROWS, ROWS)
            start = pl.multiple_of(base + inner, ROWS)
            real, imag = strip(start)
            store(start, real, imag)
            kern_ref[k, 0, pl.ds(inner, ROWS), :] = real
            kern_ref[k, 1, pl.ds(inner, ROWS), :] = imag

    plain(0, proxies)
    for k in range(entries):
        base = proxies + k * count
        kept(base, k)
        plain(base + S, count - S)
    left_re, left_im = tre[:, :S], tim[:, :S]
    cross_ref[0] = dot_tn(left_re, tre[...]) + dot_tn(left_im, tim[...])
    cross_ref[1] = dot_tn(left_re, tim[...]) - dot_tn(left_im, tre[...])


def exact(a, b, dims=((1,), (0,))):
    return lax.dot_general(a, b, (dims, ((), ())), precision=highest,
                           preferred_element_type=jnp.float32)


def solve_kernel(mine_ref, other_ref, x_ref, mat, low, high):
    n = x_ref.shape[1]
    wide = mine_ref.shape[2]
    nb = NBLK
    mat[...] = mine_ref[...] + other_ref[...]
    diagonal = lax.broadcasted_iota(jnp.int32, (n, n), 0) == lax.broadcasted_iota(
        jnp.int32, (n, n), 1
    )
    gram = mat[0, :, 0:n]
    ridge = ridge_share * jnp.sum(jnp.where(diagonal, gram, 0.0)) / n
    mat[0, :, 0:n] = gram + jnp.where(diagonal, ridge, 0.0)
    low[...] = jnp.zeros_like(low)
    high[...] = jnp.zeros_like(high)
    lane = lax.broadcasted_iota(jnp.int32, (nb, 128), 1)
    sub = lax.broadcasted_iota(jnp.int32, (nb, 128), 0)
    lane_all = lax.broadcasted_iota(jnp.int32, (n, 128), 1)
    for j in range(n // nb):
        rows = slice(j * nb, (j + 1) * nb)
        q = (j * nb) // 128 * 128
        back = (128 - (j * nb) % 128) % 128

        def turned(block, shift):
            return pltpu.roll(block, shift, 1) if shift else block

        block_re = mat[0, rows, q:q + 128]
        block_im = mat[1, rows, q:q + 128]
        re0, im0 = turned(block_re, back), turned(block_im, back)
        re1, im1 = turned(block_re, (back + nb) % 128), turned(block_im, (back + nb) % 128)
        zero = jnp.zeros_like(re0)
        m = jnp.where(lane < nb, re0, jnp.where(lane < 2 * nb, im1,
                                                jnp.where(lane - 2 * nb == sub, 1.0, zero)))
        w = jnp.where(lane < nb, -im0, jnp.where(lane < 2 * nb, re1,
                                                 jnp.where(lane - 3 * nb == sub, 1.0, zero)))
        for k in range(nb):
            col_re = m[:, k:k + 1]
            col_im = m[:, nb + k:nb + k + 1]
            scale = 1.0 / m[k:k + 1, k:k + 1]
            row_m = m[k:k + 1, :] * scale
            row_w = w[k:k + 1, :] * scale
            new_m = m - col_re * row_m - col_im * row_w
            new_w = w - col_re * row_w + col_im * row_m
            m = jnp.where(sub == k, row_m, new_m)
            w = jnp.where(sub == k, row_w, new_w)
        start = (j + 1) * nb // 128 * 128
        span = wide - start
        panel_re = mat[0, rows, start:]
        panel_im = mat[1, rows, start:]
        high[2 * nb:3 * nb, 0:span] = panel_re
        high[2 * nb:3 * nb, span:2 * span] = panel_im
        high[3 * nb:4 * nb, 0:span] = -panel_im
        high[3 * nb:4 * nb, span:2 * span] = panel_re
        solved = exact(m, high[:, 0:2 * span])
        low[0:nb, 0:2 * span] = solved
        low[nb:2 * nb, 0:span] = -solved[:, span:]
        low[nb:2 * nb, span:2 * span] = solved[:, 0:span]
        left = jnp.where(
            lane_all < nb,
            turned(mat[0, :, q:q + 128], back),
            jnp.where(lane_all < 2 * nb, turned(mat[1, :, q:q + 128], (back + nb) % 128), 0.0),
        )
        change = exact(left, low[:, 0:2 * span])
        mat[0, :, start:] = mat[0, :, start:] - change[:, 0:span]
        mat[1, :, start:] = mat[1, :, start:] - change[:, span:]
        mat[0, rows, start:] = solved[:, 0:span]
        mat[1, rows, start:] = solved[:, span:]
    x_ref[...] = mat[:, :, n:]


def update_kernel(box_count, box_total, entries, where_ref, nb_ref, kern_ref, x_ref, pivot_ref,
                  out_ref):
    n = x_ref.shape[1]
    box = where_ref[1]
    first = where_ref[2] * entries
    out_ref[...] = jnp.zeros_like(out_ref)
    xr, xi = x_ref[0], x_ref[1]
    qr, qi = pivot_ref[0:1, :], pivot_ref[1:2, :]
    nt = ((1,), (1,))
    for k in range(entries):
        slot = slot_of(nb_ref, where_ref, box, first + k, box_count, box_total)
        kr, ki = kern_ref[k, 0, :, 0:n], kern_ref[k, 1, :, 0:n]
        br = kern_ref[k, 0, :, n:] - (exact(kr, xr) - exact(ki, xi))
        bi = kern_ref[k, 1, :, n:] - (exact(kr, xi) + exact(ki, xr))
        wr = br * qr - bi * qi
        wi = br * qi + bi * qr
        out_ref[slot, 0] = out_ref[slot, 0] - (exact(wr, br, nt) - exact(wi, bi, nt))
        out_ref[slot, 1] = out_ref[slot, 1] - (exact(wr, bi, nt) + exact(wi, br, nt))


def ring(count, step):
    return [(i, (i + step) % count) for i in range(count)]


def on_device(
    box_points, proxy_directions, point_order, neighbour_boxes, neighbour_places, pivot_inverse
):
    box_count, _, point_count = box_points.shape
    col_count = lax.axis_size("col")
    box_total = lax.axis_size("box")
    col_index = lax.axis_index("col")
    box_index = lax.axis_index("box")
    group = col_count // box_count
    box = col_index // group
    part = col_index % group
    entries = neighbour_boxes.shape[1] // group
    width = pivot_inverse.shape[2]
    where = jnp.stack([box_index, box, part]).astype(jnp.int32)

    points = jnp.pad(box_points, ((0, 0), (0, 5), (0, 0)))
    order = point_order[:, None, :]

    def halo(block):
        low = lax.ppermute(block, "box", ring(box_total, 1))
        high = lax.ppermute(block, "box", ring(box_total, -1))
        return jnp.concatenate([low, block, high], axis=0)

    points = halo(points)
    order = halo(order)
    proxies = jnp.pad(proxy_directions, ((0, 5), (0, 0)))
    proxies = jnp.concatenate(
        [proxies] + [lax.ppermute(proxies, "col", ring(col_count, group * d))
                     for d in range(1, box_count)], axis=1)
    pieces = [pivot_inverse] + [lax.ppermute(pivot_inverse, "col", ring(col_count, d))
                                for d in range(1, col_count)]
    pieces = jnp.stack(pieces)
    pieces = pieces[(col_index - jnp.arange(col_count)) % col_count]
    pivots = jnp.moveaxis(lax.dynamic_index_in_dim(pieces, box, 1, keepdims=False), 0, 1)
    pivots = pivots.reshape(2, col_count * width)

    rows = proxies.shape[1] + entries * point_count
    cross, kern = pl.pallas_call(
        functools.partial(tile_kernel, box_count, box_total, entries),
        out_shape=(
            jax.ShapeDtypeStruct((2, S, point_count), jnp.float32),
            jax.ShapeDtypeStruct((entries, 2, S, point_count), jnp.float32),
        ),
        in_specs=[SMEM, SMEM, SMEM, VMEM, VMEM, VMEM],
        out_specs=(VMEM, VMEM),
        scratch_shapes=[
            pltpu.VMEM((rows, 128), jnp.float32),
            pltpu.VMEM((8, point_count), jnp.float32),
            pltpu.VMEM((rows, point_count), jnp.bfloat16),
            pltpu.VMEM((rows, point_count), jnp.bfloat16),
        ],
        compiler_params=params(),
    )(where, neighbour_boxes, neighbour_places, points, order, proxies)

    within = [(g * group + i, g * group + (i + 1) % group)
              for g in range(box_count) for i in range(group)]
    other = lax.ppermute(cross, "col", within)
    rest = point_count - S
    solved = pl.pallas_call(
        solve_kernel,
        out_shape=jax.ShapeDtypeStruct((2, S, rest), jnp.float32),
        in_specs=[VMEM, VMEM],
        out_specs=VMEM,
        scratch_shapes=[
            pltpu.VMEM((2, S, point_count), jnp.float32),
            pltpu.VMEM((128, 2 * point_count), jnp.float32),
            pltpu.VMEM((128, 2 * point_count), jnp.float32),
        ],
        compiler_params=params(),
    )(cross, other)

    mine = lax.dynamic_slice_in_dim(solved, col_index * width, width, 2)
    far = (col_index + group) % col_count
    sent = lax.dynamic_slice_in_dim(solved, far * width, width, 2)
    arrived = lax.ppermute(sent, "col", ring(col_count, group))
    interpolation = jnp.where(box == 0, jnp.stack([mine, arrived]), jnp.stack([arrived, mine]))

    buffer = pl.pallas_call(
        functools.partial(update_kernel, box_count, box_total, entries),
        out_shape=jax.ShapeDtypeStruct((3 * box_count, 2, S, S), jnp.float32),
        in_specs=[SMEM, SMEM, VMEM, VMEM, VMEM],
        out_specs=VMEM,
        compiler_params=params(),
    )(where, neighbour_boxes, kern, solved, pivots)

    reduced = lax.psum_scatter(buffer, "col", scatter_dimension=2, tiled=True)
    low = lax.ppermute(reduced[2 * box_count:], "box", ring(box_total, 1))
    high = lax.ppermute(reduced[:box_count], "box", ring(box_total, -1))
    skeleton_update = reduced[box_count:2 * box_count] + low + high
    return (interpolation, skeleton_update)


def solution(mesh):
    placed = (
        P("box", None, None),
        P(None, "col"),
        P("box", None),
        P("box", None),
        P("box", None),
        P("box", None, "col"),
    )
    return jax.shard_map(
        on_device,
        mesh=mesh,
        in_specs=placed,
        out_specs=(P("box", None, None, "col"), P("box", None, "col", None)),
        check_vma=False,
    )
```

time: 613 us -> 160 us (0.26); the launches traced: 605 us -> 159 us
  other arithmetic: 315 us -> 2.54 us
  local copies, waits for them, and re-layouts: 79.1 us -> 8.89 us
  Pallas kernels: 0 us -> 64.4 us
  matrix products: 58.5 us -> 0 us
  waiting for transfers between devices: 101 us -> 48.7 us
  loops' own time: 24.4 us -> 0 us
  starting transfers between devices: 10.9 us -> 20.7 us
    another operation x22 -> x2, other arithmetic: 235 us -> 0.76 us  [the longest x1 0.69 us: on_device(): pieces = jnp.stack(pieces)]
    pallas_call x0 -> x3, Pallas kernels: none -> 64.4 us  [the longest x1 31 us: on_device(): pl.pallas_call(solve_kernel, out_shape=jax.ShapeDtypeStruct((2, S, rest),...]
    psum x1 -> x0, waiting for transfers between devices: 47.3 us -> none  [on_device(): gram_total = lax.psum(cross_terms[:, :, :, :skel_count], 'col')]
    dot_general x22 -> x0, matrix products: 41.2 us -> none  [the longest x8 15.8 us: outer_product(): lax.dot_general(left_side, right_side, outer_dims, precision=highest, pre...]
    gather x7 -> x1, local copies, waits for them, and re-layouts: 32.4 us -> 0.57 us  [on_device(): pieces = pieces[(col_index - jnp.arange(col_count)) % col_count]]
    convert_element_type x4 -> x0, other arithmetic: 25.2 us -> none  [the longest x2 25.2 us: cross_one(): real_tile.astype(jnp.bfloat16)]
    another operation x3 -> x0, loops' own time: 24.4 us -> none  [the longest x1 20.9 us: on_device(): lax.fori_loop(0, box_count, schur_box, jnp.zeros((3 * box_count, 2, skel_...]
    neg x3 -> x0, other arithmetic: 23.4 us -> none  [the longest x2 23.3 us: cross_products(): flipped = jnp.concatenate([imag_tile, -real_tile], axis=0)]
  transfers between devices with their start and end apart: 6 -> 13, of which waited for: 6 -> 7; matrix products, arithmetic and copies ran while one was open for 0% -> 2% of each run, Pallas kernels for 0% -> 0%
where the time goes in v1:
time: 160 us; the launch traced here: 159 us
  Pallas kernels  64.4 us (40%)
  waiting for transfers between devices  48.7 us (30%)
  starting transfers between devices  20.7 us (13%)
  between operations  14.2 us (9%)
  local copies, waits for them, and re-layouts  8.89 us (6%)
  other arithmetic  2.54 us (2%)
    reduce_scatter x1, waiting for transfers between devices, on_device(): reduced = lax.psum_scatter(buffer, 'col', scatter_dimension=2, tiled=True)  36.8 us
    pallas_call x1, Pallas kernels, on_device(): pl.pallas_call(solve_kernel, out_shape=jax.ShapeDtypeStruct((2, S, rest),...  31 us
    pallas_call x1, Pallas kernels, on_device(): pl.pallas_call(functools.partial(tile_kernel, box_count, box_total, entri...  21.4 us
    pallas_call x1, Pallas kernels, on_device(): pl.pallas_call(functools.partial(update_kernel, box_count, box_total, ent...  12.1 us
    ppermute x2, starting transfers between devices, halo(): high = lax.ppermute(block, 'box', ring(box_total, -1))  7.82 us
    ppermute x1, waiting for transfers between devices, on_device(): arrived = lax.ppermute(sent, 'col', ring(col_count, group))  6.98 us
    unnamed x10, local copies, waits for them, and re-layouts  5.57 us
    ppermute x1, starting transfers between devices, on_device(): high = lax.ppermute(reduced[:box_count], 'box', ring(box_total, -1))  3.25 us
  transfers between devices with their start and end apart: 13, of which 7 were waited for; matrix products, arithmetic and copies ran while one was open for 2% of the time, Pallas kernels for 0%

profile of v1, /device:TPU:0, one launch (start us, length us, event | category | flops | bytes accessed | tf_op | source)
XLA Modules:
  0.0 159.5 jit_solution(2007111231101474956)
XLA Ops:
  7.2 0.0 reduce-scatter.2.cloned.1.call-start
  7.2 0.7 copy.10
  7.9 3.0 %collective-permute-start = (f32[2,8,512]{2,1,0:T(8,128)S(1)}, f32[2,8,512]{2,1,0:T(8,128)S(1)}, u32[]{:S(2)}, u32[]{:S(2)}) collective-permute-start(f32[2,8,512]{2,1,0:T(8,128)S(1)} %pad.8), channel_id=1, source_target_pairs={{0,4},{4,8},{8,12},{12,16},{16,20},{20,24},{24,28},{28,0},{1,5},{5... | collective-permute-start | bytes 98312 | tf_op jit(solution)/shard_map/ppermute | solution.py:251
  11.0 3.1 %collective-permute-start.1 = (f32[2,8,512]{2,1,0:T(8,128)S(1)}, f32[2,8,512]{2,1,0:T(8,128)S(1)}, u32[]{:S(2)}, u32[]{:S(2)}) collective-permute-start(f32[2,8,512]{2,1,0:T(8,128)S(1)} %pad.8), channel_id=1, source_target_pairs={{0,28},{4,0},{8,4},{12,8},{16,12},{20,16},{24,20},{28,24},{1,29},{... | collective-permute-start | bytes 98312 | tf_op jit(solution)/shard_map/ppermute | solution.py:252
  14.1 0.7 broadcast_in_dim.4
  14.8 0.0 collective-permute-start.2
  14.8 4.7 %collective-permute-start.3 = (s32[2,1,512]{2,1,0:T(1,128)S(1)}, s32[2,1,512]{2,1,0:T(1,128)S(1)}, u32[]{:S(2)}, u32[]{:S(2)}) collective-permute-start(s32[2,1,512]{2,1,0:T(1,128)S(1)} %broadcast_in_dim.4), channel_id=1, source_target_pairs={{0,28},{4,0},{8,4},{12,8},{16,12},{20,16},{24,20},{28,24},{1,29},{... | collective-permute-start | bytes 12296 | tf_op jit(solution)/shard_map/ppermute | solution.py:252
  19.5 0.7 pad.9
  20.2 1.6 collective-permute-start.4
  21.8 0.1 pad_add_fusion.1.where_ref
  21.9 0.0 collective-permute-done.2
  21.9 0.0 collective-permute-done.3
  21.9 2.0 %collective-permute-done.4 = f32[8,256]{1,0:T(8,128)S(1)} collective-permute-done((f32[8,256]{1,0:T(8,128)S(1)}, f32[8,256]{1,0:T(8,128)S(1)}, u32[]{:S(2)}, u32[]{:S(2)}) %collective-permute-start.4) | collective-permute-done | bytes 8224 | tf_op jit(solution)/shard_map/ppermute | solution.py:259
  23.8 0.0 collective-permute-done
  23.8 0.0 collective-permute-done.1
  23.9 0.0 copy-start.1
  23.9 0.7 copy-done.1
  24.6 0.0 copy-start.3
  24.6 0.7 copy-done.3
  25.2 21.4 %shard_map.77 = (f32[2,256,512]{2,1,0:T(8,128)S(1)}, f32[4,2,256,512]{3,2,1,0:T(8,128)S(1)}) custom-call(s32[3]{0:T(128)S(1)} %pad_add_fusion.1.where_ref, s32[2,8]{1,0:T(2,128)S(1)} %copy-done.1, s32[2,8]{1,0:T(2,128)S(1)} %copy-done.3, f32[6,8,512]{2,1,0:T(8,128)S(1)} %pad_maximum_fusion.points_ref, s32[6,1,512]{2,1,0:T(1,128)S(1)} %pad_add_fusion.order_ref, ...), custom_call_target="tpu_custom_call" | custom-call | tf_op jit(solution)/shard_map/pallas_call | solution.py:269
  46.6 0.0 copy-start
  46.6 1.9 %copy-done = f32[4,2,256,512]{3,2,1,0:T(8,128)} copy-done((f32[4,2,256,512]{3,2,1,0:T(8,128)}, f32[4,2,256,512]{3,2,1,0:T(8,128)S(1)}, u32[]{:S(2)}) %copy-start) | copy-done | bytes 4194328
  48.6 0.0 collective-permute-start.5
  48.6 0.5 collective-permute-start.7
  49.1 1.6 collective-permute-start.8
  50.7 1.0 collective-permute-start.9
  51.7 0.1 collective-permute-done.7
  51.8 1.1 collective-permute-done.8
  52.9 0.3 collective-permute-done.9
  53.2 0.7 pad_maximum_fusion.2
  53.9 0.6 gather_fusion
  54.5 0.1 reshape.56.pivot_ref
  54.5 0.0 collective-permute-done.5.other_ref
  54.5 31.0 %shard_map.78.x_ref = f32[2,256,256]{2,1,0:T(8,128)S(1)} custom-call(f32[2,256,512]{2,1,0:T(8,128)S(1)} %get-tuple-element.4.mine_ref, f32[2,256,512]{2,1,0:T(8,128)S(1)} %collective-permute-done.5.other_ref), custom_call_target="tpu_custom_call" | custom-call | tf_op jit(solution)/shard_map/pallas_call | solution.py:290
  85.5 0.0 copy-start.2
  85.5 0.7 copy-done.2
  86.2 12.1 %shard_map.79 = f32[6,2,256,256]{3,2,1,0:T(8,128)} custom-call(s32[3]{0:T(128)S(1)} %pad_add_fusion.1.where_ref, s32[2,8]{1,0:T(2,128)S(1)} %copy-done.2, f32[4,2,256,512]{3,2,1,0:T(8,128)} %copy-done, f32[2,256,256]{2,1,0:T(8,128)S(1)} %shard_map.78.x_ref, f32[2,256]{1,0:T(2,128)S(1)} %reshape.56.pivot_ref), custom_call_target="tpu_custom_call" | custom-call | tf_op jit(solution)/shard_map/pallas_call | solution.py:309
  98.3 0.0 reduce-scatter.2.cloned.1.call-update
  98.3 36.8 %reduce-scatter.2.cloned.1.call-done = f32[6,2,64,256]{3,2,1,0:T(8,128)} async-done(((f32[6,2,256,256]{3,2,1,0:T(8,128)}), f32[6,2,64,256]{3,2,1,0:T(8,128)}) %reduce-scatter.2.cloned.1.call-update) | async-done | bytes 786448 | tf_op jit(solution)/shard_map/reduce_scatter | solution.py:317
  135.1 1.1 fusion.3
  136.2 1.5 collective-permute-start.10
  137.7 3.3 %collective-permute-start.11 = (f32[2,2,64,256]{3,2,1,0:T(8,128)S(1)}, f32[2,2,64,256]{3,2,1,0:T(8,128)S(1)}, u32[]{:S(2)}, u32[]{:S(2)}) collective-permute-start(f32[2,2,64,256]{3,2,1,0:T(8,128)S(1)} %get-tuple-element.11), channel_id=1, source_target_pairs={{0,28},{4,0},{8,4},{12,8},{16,12},{20,16},{24,20},{28,24},{1,29},{... | collective-permute-start | bytes 786440 | tf_op jit(solution)/shard_map/ppermute | solution.py:319
  141.0 0.2 dynamic-slice_bitcast_fusion
  141.2 0.4 collective-permute-start.6
  141.6 7.0 %collective-permute-done.6 = f32[2,256,64]{2,1,0:T(8,128)S(1)} collective-permute-done((f32[2,256,64]{2,1,0:T(8,128)S(1)}, f32[2,256,64]{2,1,0:T(8,128)S(1)}, u32[]{:S(2)}, u32[]{:S(2)}) %collective-permute-start.6) | collective-permute-done | bytes 131104 | tf_op jit(solution)/shard_map/ppermute | solution.py:306
  148.6 0.9 copy.12
  149.5 0.0 collective-permute-done.10
  149.5 1.4 collective-permute-done.11
  150.9 1.7 %fusion = f32[2,2,64,256]{3,2,1,0:T(8,128)} fusion(f32[2,2,64,256]{3,2,1,0:T(8,128)S(1)} %collective-permute-done.11, f32[2,2,64,256]{3,2,1,0:T(8,128)S(1)} %collective-permute-done.10, f32[6,2,64,256]{3,2,1,0:T(8,128)} %reduce-scatter.2.cloned.1.call-done), kind=kLoop, calls=%fused_computation.3 | loop fusion | flops 131072 | bytes 1048576 | tf_op jit(solution)/shard_map/add | solution.py:320
  (9 shorter events, 0.1 us)
Async XLA Ops:
  7.2 127.9 %reduce-scatter.2.cloned.1.call-start = ((), (), s32[]{:S(2)}) async-start(), calls=%async_computation.1 | async-start | bytes 3932160 | tf_op jit(solution)/shard_map/reduce_scatter | solution.py:317
  7.9 15.9 %collective-permute-start = (f32[2,8,512]{2,1,0:T(8,128)S(1)}, f32[2,8,512]{2,1,0:T(8,128)S(1)}, u32[]{:S(2)}, u32[]{:S(2)}) collective-permute-start(f32[2,8,512]{2,1,0:T(8,128)S(1)} %pad.8), channel_id=1, source_target_pairs={{0,4},{4,8},{8,12},{12,16},{16,20},{20,24},{24,28},{28,0},{1,5},{5... | collective-permute-start | bytes 98312 | tf_op jit(solution)/shard_map/ppermute | solution.py:251
  11.0 12.9 %collective-permute-start.1 = (f32[2,8,512]{2,1,0:T(8,128)S(1)}, f32[2,8,512]{2,1,0:T(8,128)S(1)}, u32[]{:S(2)}, u32[]{:S(2)}) collective-permute-start(f32[2,8,512]{2,1,0:T(8,128)S(1)} %pad.8), channel_id=1, source_target_pairs={{0,28},{4,0},{8,4},{12,8},{16,12},{20,16},{24,20},{28,24},{1,29},{... | collective-permute-start | bytes 98312 | tf_op jit(solution)/shard_map/ppermute | solution.py:252
  14.8 7.1 %collective-permute-start.2 = (s32[2,1,512]{2,1,0:T(1,128)S(1)}, s32[2,1,512]{2,1,0:T(1,128)S(1)}, u32[]{:S(2)}, u32[]{:S(2)}) collective-permute-start(s32[2,1,512]{2,1,0:T(1,128)S(1)} %broadcast_in_dim.4), channel_id=1, source_target_pairs={{0,4},{4,8},{8,12},{12,16},{16,20},{20,24},{24,28},{28,0},{1,5},{5... | collective-permute-start | bytes 12296 | tf_op jit(solution)/shard_map/ppermute | solution.py:251
  14.8 7.1 %collective-permute-start.3 = (s32[2,1,512]{2,1,0:T(1,128)S(1)}, s32[2,1,512]{2,1,0:T(1,128)S(1)}, u32[]{:S(2)}, u32[]{:S(2)}) collective-permute-start(s32[2,1,512]{2,1,0:T(1,128)S(1)} %broadcast_in_dim.4), channel_id=1, source_target_pairs={{0,28},{4,0},{8,4},{12,8},{16,12},{20,16},{24,20},{28,24},{1,29},{... | collective-permute-start | bytes 12296 | tf_op jit(solution)/shard_map/ppermute | solution.py:252
  20.2 3.7 %collective-permute-start.4 = (f32[8,256]{1,0:T(8,128)S(1)}, f32[8,256]{1,0:T(8,128)S(1)}, u32[]{:S(2)}, u32[]{:S(2)}) collective-permute-start(f32[8,256]{1,0:T(8,128)S(1)} %pad.9), channel_id=1, source_target_pairs={{0,2},{1,3},{2,0},{3,1},{4,6},{5,7},{6,4},{7,5},{8,10},{9,11},{10,... | collective-permute-start | bytes 24584 | tf_op jit(solution)/shard_map/ppermute | solution.py:259
  23.9 0.7 copy-start.1
  24.6 0.7 copy-start.3
  46.6 2.0 %copy-start = (f32[4,2,256,512]{3,2,1,0:T(8,128)}, f32[4,2,256,512]{3,2,1,0:T(8,128)S(1)}, u32[]{:S(2)}) copy-start(f32[4,2,256,512]{3,2,1,0:T(8,128)S(1)} %get-tuple-element.5.kern_ref) | copy-start | bytes 12582916
  48.6 5.9 %collective-permute-start.5 = (f32[2,256,512]{2,1,0:T(8,128)S(1)}, f32[2,256,512]{2,1,0:T(8,128)S(1)}, u32[]{:S(2)}, u32[]{:S(2)}) collective-permute-start(f32[2,256,512]{2,1,0:T(8,128)S(1)} %get-tuple-element.4.mine_ref), channel_id=1, source_target_pairs={{0,1},{1,0},{2,3},{3,2},{4,5},{5,4},{6,7},{7,6},{8,9},{9,8},{10,11... | collective-permute-start | bytes 3145736 | tf_op jit(solution)/shard_map/ppermute | solution.py:288
  48.6 3.2 %collective-permute-start.7 = (f32[2,2,64]{2,1,0:T(2,128)}, f32[2,2,64]{2,1,0:T(2,128)S(1)}, u32[]{:S(2)}, u32[]{:S(2)}) collective-permute-start(f32[2,2,64]{2,1,0:T(2,128)} %param.11), channel_id=1, source_target_pairs={{0,1},{1,2},{2,3},{3,0},{4,5},{5,6},{6,7},{7,4},{8,9},{9,10},{10,1... | collective-permute-start | bytes 3080 | tf_op jit(solution)/shard_map/ppermute | solution.py:261
  49.1 3.8 %collective-permute-start.8 = (f32[2,2,64]{2,1,0:T(2,128)}, f32[2,2,64]{2,1,0:T(2,128)S(1)}, u32[]{:S(2)}, u32[]{:S(2)}) collective-permute-start(f32[2,2,64]{2,1,0:T(2,128)} %param.11), channel_id=1, source_target_pairs={{0,2},{1,3},{2,0},{3,1},{4,6},{5,7},{6,4},{7,5},{8,10},{9,11},{10,... | collective-permute-start | bytes 3080 | tf_op jit(solution)/shard_map/ppermute | solution.py:261
  50.7 2.5 %collective-permute-start.9 = (f32[2,2,64]{2,1,0:T(2,128)}, f32[2,2,64]{2,1,0:T(2,128)S(1)}, u32[]{:S(2)}, u32[]{:S(2)}) collective-permute-start(f32[2,2,64]{2,1,0:T(2,128)} %param.11), channel_id=1, source_target_pairs={{0,3},{1,0},{2,1},{3,2},{4,7},{5,4},{6,5},{7,6},{8,11},{9,8},{10,9... | collective-permute-start | bytes 3080 | tf_op jit(solution)/shard_map/ppermute | solution.py:261
  85.5 0.7 copy-start.2
  136.2 13.3 %collective-permute-start.10 = (f32[2,2,64,256]{3,2,1,0:T(8,128)S(1)}, f32[2,2,64,256]{3,2,1,0:T(8,128)S(1)}, u32[]{:S(2)}, u32[]{:S(2)}) collective-permute-start(f32[2,2,64,256]{3,2,1,0:T(8,128)S(1)} %get-tuple-element.10), channel_id=1, source_target_pairs={{0,4},{4,8},{8,12},{12,16},{16,20},{20,24},{24,28},{28,0},{1,5},{5... | collective-permute-start | bytes 786440 | tf_op jit(solution)/shard_map/ppermute | solution.py:318
  137.7 13.2 %collective-permute-start.11 = (f32[2,2,64,256]{3,2,1,0:T(8,128)S(1)}, f32[2,2,64,256]{3,2,1,0:T(8,128)S(1)}, u32[]{:S(2)}, u32[]{:S(2)}) collective-permute-start(f32[2,2,64,256]{3,2,1,0:T(8,128)S(1)} %get-tuple-element.11), channel_id=1, source_target_pairs={{0,28},{4,0},{8,4},{12,8},{16,12},{20,16},{24,20},{28,24},{1,29},{... | collective-permute-start | bytes 786440 | tf_op jit(solution)/shard_map/ppermute | solution.py:319
  141.2 7.4 %collective-permute-start.6 = (f32[2,256,64]{2,1,0:T(8,128)S(1)}, f32[2,256,64]{2,1,0:T(8,128)S(1)}, u32[]{:S(2)}, u32[]{:S(2)}) collective-permute-start(f32[2,256,64]{2,1,0:T(8,128)S(1)} %get-tuple-element.13), channel_id=1, source_target_pairs={{0,2},{1,3},{2,0},{3,1},{4,6},{5,7},{6,4},{7,5},{8,10},{9,11},{10,... | collective-permute-start | bytes 393224 | tf_op jit(solution)/shard_map/ppermute | solution.py:306
Sparse Core Ops, SparseCore 0:
  98.4 36.6 reduce-scatter.1

commit v2 on v1

--- a/solution.py
+++ b/solution.py
@@ -64,24 +64,31 @@
 
 
 def tile_kernel(box_count, box_total, entries, where_ref, nb_ref, place_ref, points_ref, order_ref,
-                proxy_ref, cross_ref, kern_ref, tcol, srow, tre, tim):
-    count = points_ref.shape[2]
-    proxies = proxy_ref.shape[1]
+                proxy_ref, cross_ref, kern_ref, tcol, srow, raw, tre, tim):
+    count = points_ref.shape[3]
+    share = proxy_ref.shape[2]
+    proxies = box_count * share
+    raw[...] = jnp.zeros_like(raw)
     box = where_ref[1]
     first = where_ref[2] * entries
 
     def ordered(slot):
+        side, which = slot // box_count, slot % box_count
         one_hot = (
-            lax.broadcasted_iota(jnp.int32, (count, count), 0) == order_ref[slot, 0:1, :]
+            lax.broadcasted_iota(jnp.int32, (count, count), 0)
+            == order_ref[side, pl.ds(which, 1), :]
         ).astype(jnp.float32)
+        raw[0:3, :] = points_ref[side, which]
         return lax.dot_general(
-            points_ref[slot], one_hot, (((1,), (0,)), ((), ())), precision=highest,
+            raw[...], one_hot, (((1,), (0,)), ((), ())), precision=highest,
             preferred_element_type=jnp.float32,
         )
 
     axis_row = lax.broadcasted_iota(jnp.int32, (8, count), 0)
     srow[...] = ordered(box_count + box)
-    tcol[0:proxies, 0:8] = jnp.transpose(0.5 + proxy_radius * proxy_ref[...])
+    for d in range(box_count):
+        raw[0:3, 0:share] = 0.5 + proxy_radius * proxy_ref[d]
+        tcol[d * share:(d + 1) * share, 0:8] = jnp.transpose(raw[:, 0:share])
     for k in range(entries):
         slot = slot_of(nb_ref, where_ref, box, first + k, box_count, box_total)
         code = place_ref[box, first + k]
@@ -212,7 +219,9 @@
     first = where_ref[2] * entries
     out_ref[...] = jnp.zeros_like(out_ref)
     xr, xi = x_ref[0], x_ref[1]
-    qr, qi = pivot_ref[0:1, :], pivot_ref[1:2, :]
+    pieces = range(pivot_ref.shape[0])
+    qr = jnp.concatenate([pivot_ref[c, box, 0:1, :] for c in pieces], axis=1)
+    qi = jnp.concatenate([pivot_ref[c, box, 1:2, :] for c in pieces], axis=1)
     nt = ((1,), (1,))
     for k in range(entries):
         slot = slot_of(nb_ref, where_ref, box, first + k, box_count, box_total)
@@ -223,6 +232,96 @@
         wi = br * qi + bi * qr
         out_ref[slot, 0] = out_ref[slot, 0] - (exact(wr, br, nt) - exact(wi, bi, nt))
         out_ref[slot, 1] = out_ref[slot, 1] - (exact(wr, bi, nt) + exact(wi, br, nt))
+
+
+MESH = pl.DeviceIdType.MESH
+
+
+def meet(peers):
+    barrier = pltpu.get_barrier_semaphore()
+    for peer in peers:
+        pl.semaphore_signal(barrier, inc=1, device_id=peer, device_id_type=MESH)
+    pl.semaphore_wait(barrier, len(peers))
+
+
+def exchange_kernel(box_total, col_count, group, points_ref, order_ref, proxy_ref, pivot_ref,
+                    points_out, order_out, proxy_out, pivot_out, send, recv):
+    me = lax.axis_index("col")
+    place = lax.axis_index("box")
+    after = {"box": lax.rem(place + 1, box_total)}
+    before = {"box": lax.rem(place + box_total - 1, box_total)}
+    peers = [{"col": lax.rem(me + d, col_count)} for d in range(1, col_count)]
+    meet([before, after] + peers)
+    jobs = [
+        (points_ref, points_out.at[0], after),
+        (points_ref, points_out.at[2], before),
+        (order_ref, order_out.at[0], after),
+        (order_ref, order_out.at[2], before),
+    ]
+    for d in range(1, col_count):
+        jobs.append((pivot_ref, pivot_out.at[me], peers[d - 1]))
+        if d % group == 0:
+            jobs.append((proxy_ref, proxy_out.at[d // group], peers[d - 1]))
+    copies = []
+    for i, (source, target, peer) in enumerate(jobs):
+        copy = pltpu.make_async_remote_copy(
+            src_ref=source, dst_ref=target, send_sem=send.at[i], recv_sem=recv.at[i],
+            device_id=peer, device_id_type=MESH)
+        copy.start()
+        copies.append(copy)
+    points_out[1] = points_ref[...]
+    order_out[1] = order_ref[...]
+    proxy_out[0] = proxy_ref[...]
+    pivot_out[me] = pivot_ref[...]
+    for copy in copies:
+        copy.wait()
+
+
+def reduce_kernel(box_total, col_count, group, buf_ref, out_ref, pair_in, cross_out, cross_in,
+                  held, box_in, send, recv):
+    me = lax.axis_index("col")
+    place = lax.axis_index("box")
+    partner = me + 1 - 2 * lax.rem(me, 2)
+    across = lax.rem(me + group, col_count)
+    far = lax.rem(partner + group, col_count)
+    near_id, far_id = {"col": partner}, {"col": across}
+    after = {"box": lax.rem(place + 1, box_total)}
+    before = {"box": lax.rem(place + box_total - 1, box_total)}
+    meet([near_id, far_id, before, after])
+    width = out_ref.shape[0]
+
+    def copy(index, source, target, peer):
+        one = pltpu.make_async_remote_copy(
+            src_ref=source, dst_ref=target, send_sem=send.at[index], recv_sem=recv.at[index],
+            device_id=peer, device_id_type=MESH)
+        one.start()
+        return one
+
+    turn = (0, 2, 1)
+    pairs = {}
+    for kind, block in ((0, far), (1, partner)):
+        for g in turn:
+            source = buf_ref.at[pl.ds(g * width, width), :, block]
+            pairs[g, kind] = copy(2 * g + kind, source, pair_in.at[g, kind], near_id)
+    cross = {}
+    for g in turn:
+        pairs[g, 0].wait()
+        cross_out[g] = buf_ref[g * width:(g + 1) * width, :, across] + pair_in[g, 0]
+        cross[g] = copy(6 + g, cross_out.at[g], cross_in.at[g], far_id)
+    for g in turn:
+        pairs[g, 1].wait()
+        held[g] = buf_ref[g * width:(g + 1) * width, :, me] + pair_in[g, 1]
+    moves = []
+    for side, (g, peer) in enumerate(((0, before), (2, after))):
+        cross[g].wait()
+        held[g] = held[g] + cross_in[g]
+        moves.append(copy(9 + side, held.at[g], box_in.at[side], peer))
+    cross[1].wait()
+    total = held[1] + cross_in[1]
+    moves[0].wait()
+    held[1] = total + box_in[0]
+    moves[1].wait()
+    out_ref[...] = held[1] + box_in[1]
 
 
 def ring(count, step):
@@ -244,28 +343,23 @@
     width = pivot_inverse.shape[2]
     where = jnp.stack([box_index, box, part]).astype(jnp.int32)
 
-    points = jnp.pad(box_points, ((0, 0), (0, 5), (0, 0)))
-    order = point_order[:, None, :]
-
-    def halo(block):
-        low = lax.ppermute(block, "box", ring(box_total, 1))
-        high = lax.ppermute(block, "box", ring(box_total, -1))
-        return jnp.concatenate([low, block, high], axis=0)
-
-    points = halo(points)
-    order = halo(order)
-    proxies = jnp.pad(proxy_directions, ((0, 5), (0, 0)))
-    proxies = jnp.concatenate(
-        [proxies] + [lax.ppermute(proxies, "col", ring(col_count, group * d))
-                     for d in range(1, box_count)], axis=1)
-    pieces = [pivot_inverse] + [lax.ppermute(pivot_inverse, "col", ring(col_count, d))
-                                for d in range(1, col_count)]
-    pieces = jnp.stack(pieces)
-    pieces = pieces[(col_index - jnp.arange(col_count)) % col_count]
-    pivots = jnp.moveaxis(lax.dynamic_index_in_dim(pieces, box, 1, keepdims=False), 0, 1)
-    pivots = pivots.reshape(2, col_count * width)
-
-    rows = proxies.shape[1] + entries * point_count
+    jobs = 4 + col_count - 1 + box_count - 1
+    points, order, proxies, pivots = pl.pallas_call(
+        functools.partial(exchange_kernel, box_total, col_count, group),
+        out_shape=(
+            jax.ShapeDtypeStruct((3,) + box_points.shape, jnp.float32),
+            jax.ShapeDtypeStruct((3,) + point_order.shape, jnp.int32),
+            jax.ShapeDtypeStruct((box_count,) + proxy_directions.shape, jnp.float32),
+            jax.ShapeDtypeStruct((col_count,) + pivot_inverse.shape, jnp.float32),
+        ),
+        in_specs=[VMEM] * 4,
+        out_specs=(VMEM,) * 4,
+        scratch_shapes=[pltpu.SemaphoreType.DMA((jobs,)), pltpu.SemaphoreType.DMA((jobs,))],
+        compiler_params=params(collective_id=0, has_side_effects=True),
+    )(box_points, point_order, proxy_directions, pivot_inverse)
+
+    share = proxy_directions.shape[1]
+    rows = box_count * share + entries * point_count
     cross, kern = pl.pallas_call(
         functools.partial(tile_kernel, box_count, box_total, entries),
         out_shape=(
@@ -276,6 +370,7 @@
         out_specs=(VMEM, VMEM),
         scratch_shapes=[
             pltpu.VMEM((rows, 128), jnp.float32),
+            pltpu.VMEM((8, point_count), jnp.float32),
             pltpu.VMEM((8, point_count), jnp.float32),
             pltpu.VMEM((rows, point_count), jnp.bfloat16),
             pltpu.VMEM((rows, point_count), jnp.bfloat16),
@@ -314,10 +409,24 @@
         compiler_params=params(),
     )(where, neighbour_boxes, kern, solved, pivots)
 
-    reduced = lax.psum_scatter(buffer, "col", scatter_dimension=2, tiled=True)
-    low = lax.ppermute(reduced[2 * box_count:], "box", ring(box_total, 1))
-    high = lax.ppermute(reduced[:box_count], "box", ring(box_total, -1))
-    skeleton_update = reduced[box_count:2 * box_count] + low + high
+    strip = S // col_count
+    block = (box_count, 2, strip, S)
+    skeleton_update = pl.pallas_call(
+        functools.partial(reduce_kernel, box_total, col_count, group),
+        out_shape=jax.ShapeDtypeStruct(block, jnp.float32),
+        in_specs=[VMEM],
+        out_specs=VMEM,
+        scratch_shapes=[
+            pltpu.VMEM((3, 2) + block, jnp.float32),
+            pltpu.VMEM((3,) + block, jnp.float32),
+            pltpu.VMEM((3,) + block, jnp.float32),
+            pltpu.VMEM((3,) + block, jnp.float32),
+            pltpu.VMEM((2,) + block, jnp.float32),
+            pltpu.SemaphoreType.DMA((11,)),
+            pltpu.SemaphoreType.DMA((11,)),
+        ],
+        compiler_params=params(collective_id=1, has_side_effects=True),
+    )(buffer.reshape(3 * box_count, 2, col_count, strip, S))
     return (interpolation, skeleton_update)
 
 

time: 160 us -> 112 us (0.70)
  waiting for transfers between devices: 48.7 us -> 2.66 us
  Pallas kernels: 64.4 us -> 98.8 us
  starting transfers between devices: 20.7 us -> 0.58 us
  between operations: 14.2 us -> 0.73 us
  other arithmetic: 2.54 us -> 0.11 us
    reduce_scatter x1 -> x0, waiting for transfers between devices: 36.8 us -> none  [on_device(): reduced = lax.psum_scatter(buffer, 'col', scatter_dimension=2, tiled=True)]
    pallas_call x0 -> x2, Pallas kernels: none -> 35.9 us  [the longest x1 26.4 us: on_device(): pl.pallas_call(functools.partial(reduce_kernel, box_total, col_count, gro...]
    ppermute x10 -> x0, starting transfers between devices: 20.3 us -> none  [the longest x2 7.82 us: halo(): high = lax.ppermute(block, 'box', ring(box_total, -1))]
    ppermute x1, waiting for transfers between devices: 6.98 us -> 0.01 us  [on_device(): arrived = lax.ppermute(sent, 'col', ring(col_count, group))]
    ppermute x10 -> x0, waiting for transfers between devices: 4.9 us -> none  [the longest x1 1.97 us: on_device(): lax.ppermute(proxies, 'col', ring(col_count, group * d))]
    unnamed x10 -> x17, local copies, waits for them, and re-layouts: 5.57 us -> 8.34 us
    ppermute x1, waiting for transfers between devices: 0.01 us -> 2.66 us  [on_device(): other = lax.ppermute(cross, 'col', within)]
    add x1 -> x0, other arithmetic: 1.7 us -> none  [on_device(): skeleton_update = reduced[box_count:2 * box_count] + low + high]
  transfers between devices with their start and end apart: 13 -> 2, of which waited for: 7 -> 1; matrix products, arithmetic and copies ran while one was open for 2% -> 0% of each run, Pallas kernels for 0% -> 33%
where the time goes in v2:
time: 112 us; the launch traced here: 111 us
  Pallas kernels  98.8 us (88%)
  local copies, waits for them, and re-layouts  8.55 us (8%)
  waiting for transfers between devices  2.66 us (2%)
    pallas_call x1, Pallas kernels, on_device(): pl.pallas_call(solve_kernel, out_shape=jax.ShapeDtypeStruct((2, S, rest),...  30.9 us
    pallas_call x1, Pallas kernels, on_device(): pl.pallas_call(functools.partial(reduce_kernel, box_total, col_count, gro...  26.4 us
    pallas_call x1, Pallas kernels, on_device(): pl.pallas_call(functools.partial(tile_kernel, box_count, box_total, entri...  21.6 us
    pallas_call x1, Pallas kernels, on_device(): pl.pallas_call(functools.partial(update_kernel, box_count, box_total, ent...  10.4 us
    pallas_call x1, Pallas kernels, on_device(): pl.pallas_call(functools.partial(exchange_kernel, box_total, col_count, g...  9.44 us
    unnamed x17, local copies, waits for them, and re-layouts  8.34 us
    ppermute x1, waiting for transfers between devices, on_device(): other = lax.ppermute(cross, 'col', within)  2.66 us
  transfers between devices with their start and end apart: 2, of which 1 were waited for; matrix products, arithmetic and copies ran while one was open for 0% of the time, Pallas kernels for 33%

profile of v2, /device:TPU:0, one launch (start us, length us, event | category | flops | bytes accessed | tf_op | source)
XLA Modules:
  0.0 111.4 jit_solution(16372965771975972181)
XLA Ops:
  0.6 0.7 copy.8.points_ref
  1.4 0.1 pad_add_fusion.where_ref
  1.4 0.0 copy-start.3
  1.4 0.7 copy-done.3
  2.1 0.0 copy-start.4
  2.1 0.7 copy-done.4
  2.8 0.0 copy-start.5
  2.8 0.7 copy-done.5
  3.5 9.4 %shard_map.77 = (f32[3,2,3,512]{3,2,1,0:T(4,128)S(1)}, s32[3,2,512]{2,1,0:T(2,128)S(1)}, f32[2,3,256]{2,1,0:T(4,128)S(1)}, f32[4,2,2,64]{3,2,1,0:T(2,128)S(1)}) custom-call(f32[2,3,512]{2,1,0:T(4,128)S(1)} %copy.8.points_ref, s32[2,512]{1,0:T(2,128)S(1)} %copy-done.3, f32[3,256]{1,0:T(4,128)S(1)} %copy-done.4, f32[2,2,64]{2,1,0:T(2,128)S(1)} %copy-done.5), custom_call_target="tpu_custom_call" | custom-call | tf_op jit(solution)/shard_map/pallas_call | solution.py:347
  12.9 0.0 copy-start.1
  13.0 0.7 copy-done.1
  13.6 0.0 copy-start.6
  13.6 0.7 copy-done.6
  14.3 21.6 %shard_map.78 = (f32[2,256,512]{2,1,0:T(8,128)S(1)}, f32[4,2,256,512]{3,2,1,0:T(8,128)S(1)}) custom-call(s32[3]{0:T(128)S(1)} %pad_add_fusion.where_ref, s32[2,8]{1,0:T(2,128)S(1)} %copy-done.1, s32[2,8]{1,0:T(2,128)S(1)} %copy-done.6, f32[3,2,3,512]{3,2,1,0:T(4,128)S(1)} %get-tuple-element.8.points_ref, s32[3,2,512]{2,1,0:T(2,128)S(1)} %get-tuple-element.9.order_ref, ...), custom_call_target="tpu_custom_call" | custom-call | tf_op jit(solution)/shard_map/pallas_call | solution.py:363
  35.9 0.0 copy-start
  35.9 1.9 %copy-done = f32[4,2,256,512]{3,2,1,0:T(8,128)} copy-done((f32[4,2,256,512]{3,2,1,0:T(8,128)}, f32[4,2,256,512]{3,2,1,0:T(8,128)S(1)}, u32[]{:S(2)}) %copy-start) | copy-done | bytes 4194328
  37.8 0.0 collective-permute-start
  37.8 2.7 %collective-permute-done.other_ref = f32[2,256,512]{2,1,0:T(8,128)S(1)} collective-permute-done((f32[2,256,512]{2,1,0:T(8,128)S(1)}, f32[2,256,512]{2,1,0:T(8,128)S(1)}, u32[]{:S(2)}, u32[]{:S(2)}) %collective-permute-start) | collective-permute-done | bytes 1048608 | tf_op jit(solution)/shard_map/ppermute | solution.py:383
  40.5 30.9 %shard_map.79.x_ref = f32[2,256,256]{2,1,0:T(8,128)S(1)} custom-call(f32[2,256,512]{2,1,0:T(8,128)S(1)} %get-tuple-element.11.mine_ref, f32[2,256,512]{2,1,0:T(8,128)S(1)} %collective-permute-done.other_ref), custom_call_target="tpu_custom_call" | custom-call | tf_op jit(solution)/shard_map/pallas_call | solution.py:385
  71.5 0.2 dynamic-slice_bitcast_fusion
  71.7 0.6 collective-permute-start.1
  72.2 0.0 copy-start.2
  72.2 0.7 copy-done.2
  72.9 10.4 %shard_map.80 = f32[6,2,256,256]{3,2,1,0:T(8,128)S(1)} custom-call(s32[3]{0:T(128)S(1)} %pad_add_fusion.where_ref, s32[2,8]{1,0:T(2,128)S(1)} %copy-done.2, f32[4,2,256,512]{3,2,1,0:T(8,128)} %copy-done, f32[2,256,256]{2,1,0:T(8,128)S(1)} %shard_map.79.x_ref, f32[4,2,2,64]{3,2,1,0:T(2,128)S(1)} %get-tuple-element.13.pivot_ref), custom_call_target="tpu_custom_call" | custom-call | tf_op jit(solution)/shard_map/pallas_call | solution.py:404
  83.3 26.4 %shard_map.81 = f32[2,2,64,256]{3,2,1,0:T(8,128)S(1)} custom-call(f32[6,2,4,64,256]{4,3,2,1,0:T(8,128)S(1)} %bitcast.7), custom_call_target="tpu_custom_call" | custom-call | tf_op jit(solution)/shard_map/pallas_call | solution.py:414
  109.7 0.0 collective-permute-done.1
  109.8 0.9 copy.9
  110.7 0.7 copy.11
  (1 shorter events, 0.0 us)
Async XLA Ops:
  1.4 0.7 copy-start.3
  2.1 0.7 copy-start.4
  2.8 0.7 copy-start.5
  12.9 0.7 copy-start.1
  13.6 0.7 copy-start.6
  35.9 2.0 %copy-start = (f32[4,2,256,512]{3,2,1,0:T(8,128)}, f32[4,2,256,512]{3,2,1,0:T(8,128)S(1)}, u32[]{:S(2)}) copy-start(f32[4,2,256,512]{3,2,1,0:T(8,128)S(1)} %get-tuple-element.12.kern_ref) | copy-start | bytes 12582916
  37.8 2.7 %collective-permute-start = (f32[2,256,512]{2,1,0:T(8,128)S(1)}, f32[2,256,512]{2,1,0:T(8,128)S(1)}, u32[]{:S(2)}, u32[]{:S(2)}) collective-permute-start(f32[2,256,512]{2,1,0:T(8,128)S(1)} %get-tuple-element.11.mine_ref), channel_id=1, source_target_pairs={{0,1},{1,0},{2,3},{3,2},{4,5},{5,4},{6,7},{7,6},{8,9},{9,8},{10,11... | collective-permute-start | bytes 3145736 | tf_op jit(solution)/shard_map/ppermute | solution.py:383
  71.7 38.1 %collective-permute-start.1 = (f32[2,256,64]{2,1,0:T(8,128)S(1)}, f32[2,256,64]{2,1,0:T(8,128)S(1)}, u32[]{:S(2)}, u32[]{:S(2)}) collective-permute-start(f32[2,256,64]{2,1,0:T(8,128)S(1)} %get-tuple-element.17), channel_id=1, source_target_pairs={{0,2},{1,3},{2,0},{3,1},{4,6},{5,7},{6,4},{7,5},{8,10},{9,11},{10,... | collective-permute-start | bytes 393224 | tf_op jit(solution)/shard_map/ppermute | solution.py:401
  72.2 0.7 copy-start.2

commit v3 on v2

--- a/solution.py
+++ b/solution.py
@@ -17,10 +17,8 @@
 NBLK = 32
 ROWS = 32
 
-COS = (1.0, -19.73920440673828, 64.93911743164062, -85.45014190673828, 60.16762924194336,
-       -25.967599868774414, 6.528658390045166)
-SIN = (6.2831854820251465, -41.34170150756836, 81.60513305664062, -76.70301818847656,
-       42.02592849731445, -14.899847030639648, 3.2381374835968018)
+COS = (1.4142135381698608, -6.978850841522217, 5.739460468292236, -1.883557915687561, 0.3106880187988281)
+SIN = (4.442883014678955, -7.308245658874512, 3.606354236602783, -0.8461116552352905, 0.1098245158791542)
 
 VMEM = pl.BlockSpec(memory_space=pltpu.VMEM)
 SMEM = pl.BlockSpec(memory_space=pltpu.SMEM)
@@ -41,14 +39,15 @@
     dx = tx - sx
     dy = ty - sy
     dz = tz - sz
-    square = dx * dx + dy * dy + dz * dz + softening * softening
+    square = (dx * dx + dy * dy) + (dz * dz + 4.0 * softening * softening)
     inverse = lax.rsqrt(square)
-    inverse = inverse * (1.5 - 0.5 * square * inverse * inverse)
-    turns = 2.0 * (square * inverse)
+    turns = square * inverse
     part = turns - jnp.floor(turns + 0.5)
     z = part * part
-    amplitude = inverse * (1.0 / (4.0 * math.pi))
-    return amplitude * horner(COS, z), (amplitude * part) * horner(SIN, z)
+    amplitude = inverse * (1.0 / (2.0 * math.pi))
+    sine = part * horner(SIN, z)
+    scaled = amplitude * sine
+    return amplitude - scaled * sine, scaled * horner(COS, z)
 
 
 def slot_of(nb_ref, where_ref, row, entry, box_count, box_total):
@@ -85,9 +84,9 @@
         )
 
     axis_row = lax.broadcasted_iota(jnp.int32, (8, count), 0)
-    srow[...] = ordered(box_count + box)
+    srow[...] = 2.0 * ordered(box_count + box)
     for d in range(box_count):
-        raw[0:3, 0:share] = 0.5 + proxy_radius * proxy_ref[d]
+        raw[0:3, 0:share] = 2.0 * (0.5 + proxy_radius * proxy_ref[d])
         tcol[d * share:(d + 1) * share, 0:8] = jnp.transpose(raw[:, 0:share])
     for k in range(entries):
         slot = slot_of(nb_ref, where_ref, box, first + k, box_count, box_total)
@@ -100,7 +99,7 @@
             jnp.where(axis_row == 1, shift[1].astype(jnp.float32), shift[2].astype(jnp.float32)),
         )
         start = proxies + k * count
-        tcol[start:start + count, 0:8] = jnp.transpose(ordered(slot) + move)
+        tcol[start:start + count, 0:8] = jnp.transpose(2.0 * (ordered(slot) + move))
 
     def strip(start):
         return kernel_values(
@@ -160,16 +159,11 @@
     lane = lax.broadcasted_iota(jnp.int32, (nb, 128), 1)
     sub = lax.broadcasted_iota(jnp.int32, (nb, 128), 0)
     lane_all = lax.broadcasted_iota(jnp.int32, (n, 128), 1)
-    for j in range(n // nb):
-        rows = slice(j * nb, (j + 1) * nb)
-        q = (j * nb) // 128 * 128
-        back = (128 - (j * nb) % 128) % 128
-
-        def turned(block, shift):
-            return pltpu.roll(block, shift, 1) if shift else block
-
-        block_re = mat[0, rows, q:q + 128]
-        block_im = mat[1, rows, q:q + 128]
+
+    def turned(block, shift):
+        return pltpu.roll(block, shift, 1) if shift else block
+
+    def inverse(block_re, block_im, back):
         re0, im0 = turned(block_re, back), turned(block_im, back)
         re1, im1 = turned(block_re, (back + nb) % 128), turned(block_im, (back + nb) % 128)
         zero = jnp.zeros_like(re0)
@@ -177,16 +171,33 @@
                                                 jnp.where(lane - 2 * nb == sub, 1.0, zero)))
         w = jnp.where(lane < nb, -im0, jnp.where(lane < 2 * nb, re1,
                                                  jnp.where(lane - 3 * nb == sub, 1.0, zero)))
-        for k in range(nb):
-            col_re = m[:, k:k + 1]
-            col_im = m[:, nb + k:nb + k + 1]
-            scale = 1.0 / m[k:k + 1, k:k + 1]
-            row_m = m[k:k + 1, :] * scale
-            row_w = w[k:k + 1, :] * scale
-            new_m = m - col_re * row_m - col_im * row_w
-            new_w = w - col_re * row_w + col_im * row_m
-            m = jnp.where(sub == k, row_m, new_m)
-            w = jnp.where(sub == k, row_w, new_w)
+
+        def spread(block, k):
+            return jnp.broadcast_to(block[:, k:k + 1], (nb, 128))
+
+        for k in range(0, nb, 2):
+            p0, p1 = spread(m, k), spread(m, k + 1)
+            s0, s1 = spread(m, nb + k), spread(m, nb + k + 1)
+            a, d = p0[k:k + 1], p1[k + 1:k + 2]
+            br, bi = p1[k:k + 1], s1[k:k + 1]
+            scale = 1.0 / (a * d - (br * br + bi * bi))
+            m0, m1, w0, w1 = m[k:k + 1], m[k + 1:k + 2], w[k:k + 1], w[k + 1:k + 2]
+            row_m0 = (d * m0 - (br * m1 + bi * w1)) * scale
+            row_w0 = (d * w0 - (br * w1 - bi * m1)) * scale
+            row_m1 = (a * m1 - (br * m0 - bi * w0)) * scale
+            row_w1 = (a * w1 - (br * w0 + bi * m0)) * scale
+            new_m = m - ((p0 * row_m0 + s0 * row_w0) + (p1 * row_m1 + s1 * row_w1))
+            new_w = w - ((p0 * row_w0 - s0 * row_m0) + (p1 * row_w1 - s1 * row_m1))
+            m = jnp.where(sub == k, row_m0, jnp.where(sub == k + 1, row_m1, new_m))
+            w = jnp.where(sub == k, row_w0, jnp.where(sub == k + 1, row_w1, new_w))
+        return m
+
+    m = inverse(mat[0, 0:nb, 0:128], mat[1, 0:nb, 0:128], 0)
+    for j in range(n // nb):
+        rows = slice(j * nb, (j + 1) * nb)
+        after = slice((j + 1) * nb, (j + 2) * nb)
+        q = (j * nb) // 128 * 128
+        back = (128 - (j * nb) % 128) % 128
         start = (j + 1) * nb // 128 * 128
         span = wide - start
         panel_re = mat[0, rows, start:]
@@ -204,12 +215,29 @@
             turned(mat[0, :, q:q + 128], back),
             jnp.where(lane_all < 2 * nb, turned(mat[1, :, q:q + 128], (back + nb) % 128), 0.0),
         )
+        if (j + 1) * nb < n:
+            ahead = left[after]
+            next_re = mat[0, after, start:start + 128] - exact(ahead, low[:, 0:128])
+            next_im = mat[1, after, start:start + 128] - exact(ahead, low[:, span:span + 128])
+            m = inverse(next_re, next_im, (128 - ((j + 1) * nb) % 128) % 128)
         change = exact(left, low[:, 0:2 * span])
         mat[0, :, start:] = mat[0, :, start:] - change[:, 0:span]
         mat[1, :, start:] = mat[1, :, start:] - change[:, span:]
         mat[0, rows, start:] = solved[:, 0:span]
         mat[1, rows, start:] = solved[:, span:]
     x_ref[...] = mat[:, :, n:]
+
+
+def split(x):
+    high = x.astype(jnp.bfloat16)
+    return high, (x - high.astype(jnp.float32)).astype(jnp.bfloat16)
+
+
+def threefold(a, b, dims=((1,), (0,))):
+    def one(x, y):
+        return lax.dot_general(x, y, (dims, ((), ())), preferred_element_type=jnp.float32)
+
+    return one(a[0], b[0]) + (one(a[0], b[1]) + one(a[1], b[0]))
 
 
 def update_kernel(box_count, box_total, entries, where_ref, nb_ref, kern_ref, x_ref, pivot_ref,
@@ -219,19 +247,23 @@
     first = where_ref[2] * entries
     out_ref[...] = jnp.zeros_like(out_ref)
     xr, xi = x_ref[0], x_ref[1]
+    right = split(jnp.concatenate(
+        [jnp.concatenate([xr, xi], axis=1), jnp.concatenate([-xi, xr], axis=1)], axis=0))
     pieces = range(pivot_ref.shape[0])
     qr = jnp.concatenate([pivot_ref[c, box, 0:1, :] for c in pieces], axis=1)
     qi = jnp.concatenate([pivot_ref[c, box, 1:2, :] for c in pieces], axis=1)
     nt = ((1,), (1,))
     for k in range(entries):
         slot = slot_of(nb_ref, where_ref, box, first + k, box_count, box_total)
-        kr, ki = kern_ref[k, 0, :, 0:n], kern_ref[k, 1, :, 0:n]
-        br = kern_ref[k, 0, :, n:] - (exact(kr, xr) - exact(ki, xi))
-        bi = kern_ref[k, 1, :, n:] - (exact(kr, xi) + exact(ki, xr))
-        wr = br * qr - bi * qi
-        wi = br * qi + bi * qr
-        out_ref[slot, 0] = out_ref[slot, 0] - (exact(wr, br, nt) - exact(wi, bi, nt))
-        out_ref[slot, 1] = out_ref[slot, 1] - (exact(wr, bi, nt) + exact(wi, br, nt))
+        left = split(jnp.concatenate([kern_ref[k, 0, :, 0:n], kern_ref[k, 1, :, 0:n]], axis=1))
+        both = threefold(left, right)
+        br = kern_ref[k, 0, :, n:] - both[:, 0:n]
+        bi = kern_ref[k, 1, :, n:] - both[:, n:]
+        wr = split(br * qr - bi * qi)
+        wi = split(br * qi + bi * qr)
+        sr, si = split(br), split(bi)
+        out_ref[slot, 0] = out_ref[slot, 0] - (threefold(wr, sr, nt) - threefold(wi, si, nt))
+        out_ref[slot, 1] = out_ref[slot, 1] - (threefold(wr, si, nt) + threefold(wi, sr, nt))
 
 
 MESH = pl.DeviceIdType.MESH
@@ -245,7 +277,7 @@
 
 
 def exchange_kernel(box_total, col_count, group, points_ref, order_ref, proxy_ref, pivot_ref,
-                    points_out, order_out, proxy_out, pivot_out, send, recv):
+                    points_out, order_out, proxy_out, pivot_out, send, recv, local):
     me = lax.axis_index("col")
     place = lax.axis_index("box")
     after = {"box": lax.rem(place + 1, box_total)}
@@ -269,10 +301,12 @@
             device_id=peer, device_id_type=MESH)
         copy.start()
         copies.append(copy)
-    points_out[1] = points_ref[...]
-    order_out[1] = order_ref[...]
-    proxy_out[0] = proxy_ref[...]
-    pivot_out[me] = pivot_ref[...]
+    own = ((points_ref, points_out.at[1]), (order_ref, order_out.at[1]),
+           (proxy_ref, proxy_out.at[0]), (pivot_ref, pivot_out.at[me]))
+    for i, (source, target) in enumerate(own):
+        copy = pltpu.make_async_copy(source, target, local.at[i])
+        copy.start()
+        copies.append(copy)
     for copy in copies:
         copy.wait()
 
@@ -352,9 +386,10 @@
             jax.ShapeDtypeStruct((box_count,) + proxy_directions.shape, jnp.float32),
             jax.ShapeDtypeStruct((col_count,) + pivot_inverse.shape, jnp.float32),
         ),
-        in_specs=[VMEM] * 4,
+        in_specs=[pl.BlockSpec(memory_space=pl.ANY)] * 4,
         out_specs=(VMEM,) * 4,
-        scratch_shapes=[pltpu.SemaphoreType.DMA((jobs,)), pltpu.SemaphoreType.DMA((jobs,))],
+        scratch_shapes=[pltpu.SemaphoreType.DMA((jobs,)), pltpu.SemaphoreType.DMA((jobs,)),
+                        pltpu.SemaphoreType.DMA((4,))],
         compiler_params=params(collective_id=0, has_side_effects=True),
     )(box_points, point_order, proxy_directions, pivot_inverse)
 

time: 112 us -> 93 us (0.83)
  Pallas kernels: 98.8 us -> 80 us
    pallas_call x1, Pallas kernels: 30.9 us -> 18 us  [on_device(): pl.pallas_call(solve_kernel, out_shape=jax.ShapeDtypeStruct((2, S, rest),...]
    pallas_call x1, Pallas kernels: 10.4 us -> 6.9 us  [on_device(): pl.pallas_call(functools.partial(update_kernel, box_count, box_total, ent...]
    pallas_call x1, Pallas kernels: 21.6 us -> 19.2 us  [on_device(): pl.pallas_call(functools.partial(tile_kernel, box_count, box_total, entri...]
  transfers between devices with their start and end apart: 2 -> 2, of which waited for: 1 -> 1; matrix products, arithmetic and copies ran while one was open for 0% -> 0% of each run, Pallas kernels for 33% -> 36%
where the time goes in v3:
time: 93 us; the launch traced here: 92.6 us
  Pallas kernels  80 us (86%)
  local copies, waits for them, and re-layouts  8.55 us (9%)
  waiting for transfers between devices  2.66 us (3%)
    pallas_call x1, Pallas kernels, on_device(): pl.pallas_call(functools.partial(reduce_kernel, box_total, col_count, gro...  26.4 us
    pallas_call x1, Pallas kernels, on_device(): pl.pallas_call(functools.partial(tile_kernel, box_count, box_total, entri...  19.2 us
    pallas_call x1, Pallas kernels, on_device(): pl.pallas_call(solve_kernel, out_shape=jax.ShapeDtypeStruct((2, S, rest),...  18 us
    pallas_call x1, Pallas kernels, on_device(): pl.pallas_call(functools.partial(exchange_kernel, box_total, col_count, g...  9.48 us
    unnamed x17, local copies, waits for them, and re-layouts  8.34 us
    pallas_call x1, Pallas kernels, on_device(): pl.pallas_call(functools.partial(update_kernel, box_count, box_total, ent...  6.9 us
    ppermute x1, waiting for transfers between devices, on_device(): other = lax.ppermute(cross, 'col', within)  2.66 us
  transfers between devices with their start and end apart: 2, of which 1 were waited for; matrix products, arithmetic and copies ran while one was open for 0% of the time, Pallas kernels for 36%

profile of v3, /device:TPU:0, one launch (start us, length us, event | category | flops | bytes accessed | tf_op | source)
XLA Modules:
  0.0 92.6 jit_solution(7303029354710005019)
XLA Ops:
  0.6 0.7 copy.8.points_ref
  1.4 0.1 pad_add_fusion.where_ref
  1.4 0.0 copy-start.3
  1.4 0.7 copy-done.3
  2.1 0.0 copy-start.4
  2.1 0.7 copy-done.4
  2.8 0.0 copy-start.5
  2.8 0.7 copy-done.5
  3.5 9.5 %shard_map.77 = (f32[3,2,3,512]{3,2,1,0:T(4,128)S(1)}, s32[3,2,512]{2,1,0:T(2,128)S(1)}, f32[2,3,256]{2,1,0:T(4,128)S(1)}, f32[4,2,2,64]{3,2,1,0:T(2,128)S(1)}) custom-call(f32[2,3,512]{2,1,0:T(4,128)S(1)} %copy.8.points_ref, s32[2,512]{1,0:T(2,128)S(1)} %copy-done.3, f32[3,256]{1,0:T(4,128)S(1)} %copy-done.4, f32[2,2,64]{2,1,0:T(2,128)S(1)} %copy-done.5), custom_call_target="tpu_custom_call" | custom-call | tf_op jit(solution)/shard_map/pallas_call | solution.py:381
  13.0 0.0 copy-start.1
  13.0 0.7 copy-done.1
  13.7 0.0 copy-start.6
  13.7 0.7 copy-done.6
  14.3 19.2 %shard_map.78 = (f32[2,256,512]{2,1,0:T(8,128)S(1)}, f32[4,2,256,512]{3,2,1,0:T(8,128)S(1)}) custom-call(s32[3]{0:T(128)S(1)} %pad_add_fusion.where_ref, s32[2,8]{1,0:T(2,128)S(1)} %copy-done.1, s32[2,8]{1,0:T(2,128)S(1)} %copy-done.6, f32[3,2,3,512]{3,2,1,0:T(4,128)S(1)} %get-tuple-element.8.points_ref, s32[3,2,512]{2,1,0:T(2,128)S(1)} %get-tuple-element.9.order_ref, ...), custom_call_target="tpu_custom_call" | custom-call | tf_op jit(solution)/shard_map/pallas_call | solution.py:398
  33.6 0.0 copy-start
  33.6 1.9 %copy-done = f32[4,2,256,512]{3,2,1,0:T(8,128)} copy-done((f32[4,2,256,512]{3,2,1,0:T(8,128)}, f32[4,2,256,512]{3,2,1,0:T(8,128)S(1)}, u32[]{:S(2)}) %copy-start) | copy-done | bytes 4194328
  35.6 0.0 collective-permute-start
  35.6 2.7 %collective-permute-done.other_ref = f32[2,256,512]{2,1,0:T(8,128)S(1)} collective-permute-done((f32[2,256,512]{2,1,0:T(8,128)S(1)}, f32[2,256,512]{2,1,0:T(8,128)S(1)}, u32[]{:S(2)}, u32[]{:S(2)}) %collective-permute-start) | collective-permute-done | bytes 1048608 | tf_op jit(solution)/shard_map/ppermute | solution.py:418
  38.2 18.0 %shard_map.79.x_ref = f32[2,256,256]{2,1,0:T(8,128)S(1)} custom-call(f32[2,256,512]{2,1,0:T(8,128)S(1)} %get-tuple-element.11.mine_ref, f32[2,256,512]{2,1,0:T(8,128)S(1)} %collective-permute-done.other_ref), custom_call_target="tpu_custom_call" | custom-call | tf_op jit(solution)/shard_map/pallas_call | solution.py:420
  56.2 0.2 dynamic-slice_bitcast_fusion
  56.4 0.6 collective-permute-start.1
  57.0 0.0 copy-start.2
  57.0 0.7 copy-done.2
  57.7 6.9 %shard_map.80 = f32[6,2,256,256]{3,2,1,0:T(8,128)S(1)} custom-call(s32[3]{0:T(128)S(1)} %pad_add_fusion.where_ref, s32[2,8]{1,0:T(2,128)S(1)} %copy-done.2, f32[4,2,256,512]{3,2,1,0:T(8,128)} %copy-done, f32[2,256,256]{2,1,0:T(8,128)S(1)} %shard_map.79.x_ref, f32[4,2,2,64]{3,2,1,0:T(2,128)S(1)} %get-tuple-element.13.pivot_ref), custom_call_target="tpu_custom_call" | custom-call | tf_op jit(solution)/shard_map/pallas_call | solution.py:439
  64.6 26.4 %shard_map.81 = f32[2,2,64,256]{3,2,1,0:T(8,128)S(1)} custom-call(f32[6,2,4,64,256]{4,3,2,1,0:T(8,128)S(1)} %bitcast.7), custom_call_target="tpu_custom_call" | custom-call | tf_op jit(solution)/shard_map/pallas_call | solution.py:449
  91.0 0.0 collective-permute-done.1
  91.1 0.9 copy.9
  91.9 0.7 copy.11
  (1 shorter events, 0.0 us)
Async XLA Ops:
  1.4 0.7 copy-start.3
  2.1 0.7 copy-start.4
  2.8 0.7 copy-start.5
  13.0 0.7 copy-start.1
  13.7 0.7 copy-start.6
  33.6 2.0 %copy-start = (f32[4,2,256,512]{3,2,1,0:T(8,128)}, f32[4,2,256,512]{3,2,1,0:T(8,128)S(1)}, u32[]{:S(2)}) copy-start(f32[4,2,256,512]{3,2,1,0:T(8,128)S(1)} %get-tuple-element.12.kern_ref) | copy-start | bytes 12582916
  35.6 2.7 %collective-permute-start = (f32[2,256,512]{2,1,0:T(8,128)S(1)}, f32[2,256,512]{2,1,0:T(8,128)S(1)}, u32[]{:S(2)}, u32[]{:S(2)}) collective-permute-start(f32[2,256,512]{2,1,0:T(8,128)S(1)} %get-tuple-element.11.mine_ref), channel_id=1, source_target_pairs={{0,1},{1,0},{2,3},{3,2},{4,5},{5,4},{6,7},{7,6},{8,9},{9,8},{10,11... | collective-permute-start | bytes 3145736 | tf_op jit(solution)/shard_map/ppermute | solution.py:418
  56.4 34.6 %collective-permute-start.1 = (f32[2,256,64]{2,1,0:T(8,128)S(1)}, f32[2,256,64]{2,1,0:T(8,128)S(1)}, u32[]{:S(2)}, u32[]{:S(2)}) collective-permute-start(f32[2,256,64]{2,1,0:T(8,128)S(1)} %get-tuple-element.17), channel_id=1, source_target_pairs={{0,2},{1,3},{2,0},{3,1},{4,6},{5,7},{6,4},{7,5},{8,10},{9,11},{10,... | collective-permute-start | bytes 393224 | tf_op jit(solution)/shard_map/ppermute | solution.py:436
  57.0 0.7 copy-start.2

commit v4 on v3

--- a/solution.py
+++ b/solution.py
@@ -15,7 +15,7 @@
 ridge_share = 0.05
 highest = lax.Precision.HIGHEST
 NBLK = 32
-ROWS = 32
+ROWS = 16
 
 COS = (1.4142135381698608, -6.978850841522217, 5.739460468292236, -1.883557915687561, 0.3106880187988281)
 SIN = (4.442883014678955, -7.308245658874512, 3.606354236602783, -0.8461116552352905, 0.1098245158791542)
@@ -63,7 +63,7 @@
 
 
 def tile_kernel(box_count, box_total, entries, where_ref, nb_ref, place_ref, points_ref, order_ref,
-                proxy_ref, cross_ref, kern_ref, tcol, srow, raw, tre, tim):
+                proxy_ref, cross_ref, kern_ref, tcol, srow, raw, tiles, total):
     count = points_ref.shape[3]
     share = proxy_ref.shape[2]
     proxies = box_count * share
@@ -76,18 +76,17 @@
         one_hot = (
             lax.broadcasted_iota(jnp.int32, (count, count), 0)
             == order_ref[side, pl.ds(which, 1), :]
-        ).astype(jnp.float32)
+        ).astype(jnp.float32).astype(jnp.bfloat16)
         raw[0:3, :] = points_ref[side, which]
-        return lax.dot_general(
-            raw[...], one_hot, (((1,), (0,)), ((), ())), precision=highest,
-            preferred_element_type=jnp.float32,
-        )
+        whole = raw[...]
+        top = whole.astype(jnp.bfloat16).astype(jnp.float32)
+        mid = (whole - top).astype(jnp.bfloat16).astype(jnp.float32)
+        rows = jnp.concatenate([top, mid, whole - top - mid, jnp.zeros_like(top)], axis=0)
+        picked = jnp.dot(rows.astype(jnp.bfloat16), one_hot, preferred_element_type=jnp.float32)
+        return (picked[0:8] + picked[8:16]) + picked[16:24]
 
     axis_row = lax.broadcasted_iota(jnp.int32, (8, count), 0)
     srow[...] = 2.0 * ordered(box_count + box)
-    for d in range(box_count):
-        raw[0:3, 0:share] = 2.0 * (0.5 + proxy_radius * proxy_ref[d])
-        tcol[d * share:(d + 1) * share, 0:8] = jnp.transpose(raw[:, 0:share])
     for k in range(entries):
         slot = slot_of(nb_ref, where_ref, box, first + k, box_count, box_total)
         code = place_ref[box, first + k]
@@ -100,42 +99,55 @@
         )
         start = proxies + k * count
         tcol[start:start + count, 0:8] = jnp.transpose(2.0 * (ordered(slot) + move))
-
-    def strip(start):
-        return kernel_values(
-            tcol[pl.ds(start, ROWS), 0:1], tcol[pl.ds(start, ROWS), 1:2],
-            tcol[pl.ds(start, ROWS), 2:3], srow[0:1, :], srow[1:2, :], srow[2:3, :],
-        )
-
-    def store(start, real, imag):
-        tre[pl.ds(start, ROWS), :] = real.astype(jnp.bfloat16)
-        tim[pl.ds(start, ROWS), :] = imag.astype(jnp.bfloat16)
-
-    def plain(base, rows):
-        @pl.loop(0, rows // ROWS)
-        def _(i):
+    for d in range(box_count):
+        raw[0:3, 0:share] = 2.0 * (0.5 + proxy_radius * proxy_ref[d])
+        tcol[d * share:(d + 1) * share, 0:8] = jnp.transpose(raw[:, 0:share])
+    block = tiles.shape[1] // 2
+
+    def evaluate(base, slot, keep=None):
+        for i in range(block // ROWS):
+            inner = slice(i * ROWS, (i + 1) * ROWS)
+            lower = slice(block + i * ROWS, block + (i + 1) * ROWS)
             start = pl.multiple_of(base + i * ROWS, ROWS)
-            real, imag = strip(start)
-            store(start, real, imag)
-
-    def kept(base, k):
-        @pl.loop(0, S // ROWS)
-        def _(i):
-            inner = pl.multiple_of(i * ROWS, ROWS)
-            start = pl.multiple_of(base + inner, ROWS)
-            real, imag = strip(start)
-            store(start, real, imag)
-            kern_ref[k, 0, pl.ds(inner, ROWS), :] = real
-            kern_ref[k, 1, pl.ds(inner, ROWS), :] = imag
-
-    plain(0, proxies)
-    for k in range(entries):
+            tx = tcol[pl.ds(start, ROWS), 0:1]
+            ty = tcol[pl.ds(start, ROWS), 1:2]
+            tz = tcol[pl.ds(start, ROWS), 2:3]
+            for c in range(0, count, 256):
+                here = slice(c, c + 256)
+                there = slice(count + c, count + c + 256)
+                real, imag = kernel_values(tx, ty, tz, srow[0:1, here], srow[1:2, here],
+                                           srow[2:3, here])
+                if keep is not None:
+                    kern_ref[keep, 0, inner, here] = real
+                    kern_ref[keep, 1, inner, here] = imag
+                real = real.astype(jnp.bfloat16)
+                imag = imag.astype(jnp.bfloat16)
+                tiles[slot, inner, here] = real
+                tiles[slot, inner, there] = imag
+                tiles[slot, lower, here] = imag
+                tiles[slot, lower, there] = -real
+
+    def gather(slot):
+        total[...] += dot_tn(tiles[slot, :, 0:S], tiles[slot])
+
+    total[...] = jnp.zeros_like(total)
+    evaluate(0, 0)
+    for i in range(1, proxies // block):
+        gather((i + 1) % 2)
+        evaluate(i * block, i % 2)
+    parity = (proxies // block) % 2
+    per = count // block
+
+    @pl.loop(0, entries)
+    def _(k):
         base = proxies + k * count
-        kept(base, k)
-        plain(base + S, count - S)
-    left_re, left_im = tre[:, :S], tim[:, :S]
-    cross_ref[0] = dot_tn(left_re, tre[...]) + dot_tn(left_im, tim[...])
-    cross_ref[1] = dot_tn(left_re, tim[...]) - dot_tn(left_im, tre[...])
+        for i in range(per):
+            gather((parity + i + 1) % 2)
+            evaluate(base + i * block, (parity + i) % 2, k if i == 0 else None)
+
+    gather((parity + per - 1) % 2)
+    cross_ref[0] = total[:, 0:count]
+    cross_ref[1] = total[:, count:]
 
 
 def exact(a, b, dims=((1,), (0,))):
@@ -311,6 +323,21 @@
         copy.wait()
 
 
+def swap_kernel(mine_ref, other_ref, send, recv):
+    me = lax.axis_index("col")
+    peer = {"col": me + 1 - 2 * lax.rem(me, 2)}
+    meet([peer])
+    copies = []
+    for i in range(mine_ref.shape[0]):
+        copy = pltpu.make_async_remote_copy(
+            src_ref=mine_ref.at[i], dst_ref=other_ref.at[i], send_sem=send.at[i],
+            recv_sem=recv.at[i], device_id=peer, device_id_type=MESH)
+        copy.start()
+        copies.append(copy)
+    for copy in copies:
+        copy.wait()
+
+
 def reduce_kernel(box_total, col_count, group, buf_ref, out_ref, pair_in, cross_out, cross_in,
                   held, box_in, send, recv):
     me = lax.axis_index("col")
@@ -331,29 +358,37 @@
         one.start()
         return one
 
-    turn = (0, 2, 1)
+    box = me // group
+    fed = 1 - box
     pairs = {}
     for kind, block in ((0, far), (1, partner)):
-        for g in turn:
+        for g in (0, 2):
             source = buf_ref.at[pl.ds(g * width, width), :, block]
             pairs[g, kind] = copy(2 * g + kind, source, pair_in.at[g, kind], near_id)
+        pairs[1, kind] = copy(2 + kind, buf_ref.at[width + fed, :, block],
+                              pair_in.at[1, kind, 0], near_id)
     cross = {}
-    for g in turn:
+    for g in (0, 2):
         pairs[g, 0].wait()
         cross_out[g] = buf_ref[g * width:(g + 1) * width, :, across] + pair_in[g, 0]
         cross[g] = copy(6 + g, cross_out.at[g], cross_in.at[g], far_id)
-    for g in turn:
+    pairs[1, 0].wait()
+    cross_out[1, 0] = buf_ref[width + fed, :, across] + pair_in[1, 0, 0]
+    cross[1] = copy(7, cross_out.at[1, 0], cross_in.at[1, 0], far_id)
+    for g in (0, 2):
         pairs[g, 1].wait()
         held[g] = buf_ref[g * width:(g + 1) * width, :, me] + pair_in[g, 1]
+    pairs[1, 1].wait()
+    held[1, fed] = buf_ref[width + fed, :, me] + pair_in[1, 1, 0]
     moves = []
     for side, (g, peer) in enumerate(((0, before), (2, after))):
         cross[g].wait()
         held[g] = held[g] + cross_in[g]
         moves.append(copy(9 + side, held.at[g], box_in.at[side], peer))
     cross[1].wait()
-    total = held[1] + cross_in[1]
+    held[1, box] = cross_in[1, 0]
     moves[0].wait()
-    held[1] = total + box_in[0]
+    held[1] = held[1] + box_in[0]
     moves[1].wait()
     out_ref[...] = held[1] + box_in[1]
 
@@ -390,7 +425,7 @@
         out_specs=(VMEM,) * 4,
         scratch_shapes=[pltpu.SemaphoreType.DMA((jobs,)), pltpu.SemaphoreType.DMA((jobs,)),
                         pltpu.SemaphoreType.DMA((4,))],
-        compiler_params=params(collective_id=0, has_side_effects=True),
+        compiler_params=pltpu.CompilerParams(collective_id=0, has_side_effects=True),
     )(box_points, point_order, proxy_directions, pivot_inverse)
 
     share = proxy_directions.shape[1]
@@ -407,15 +442,20 @@
             pltpu.VMEM((rows, 128), jnp.float32),
             pltpu.VMEM((8, point_count), jnp.float32),
             pltpu.VMEM((8, point_count), jnp.float32),
-            pltpu.VMEM((rows, point_count), jnp.bfloat16),
-            pltpu.VMEM((rows, point_count), jnp.bfloat16),
+            pltpu.VMEM((2, 2 * S, 2 * point_count), jnp.bfloat16),
+            pltpu.VMEM((S, 2 * point_count), jnp.float32),
         ],
         compiler_params=params(),
     )(where, neighbour_boxes, neighbour_places, points, order, proxies)
 
-    within = [(g * group + i, g * group + (i + 1) % group)
-              for g in range(box_count) for i in range(group)]
-    other = lax.ppermute(cross, "col", within)
+    other = pl.pallas_call(
+        swap_kernel,
+        out_shape=jax.ShapeDtypeStruct(cross.shape, jnp.float32),
+        in_specs=[VMEM],
+        out_specs=VMEM,
+        scratch_shapes=[pltpu.SemaphoreType.DMA((2,)), pltpu.SemaphoreType.DMA((2,))],
+        compiler_params=params(collective_id=2, has_side_effects=True),
+    )(cross)
     rest = point_count - S
     solved = pl.pallas_call(
         solve_kernel,

time: 93 us -> 85.8 us (0.923)
  Pallas kernels: 80 us -> 75.3 us
  waiting for transfers between devices: 2.66 us -> 0.01 us
    pallas_call x1, Pallas kernels: 19.2 us -> 11 us  [on_device(): pl.pallas_call(functools.partial(tile_kernel, box_count, box_total, entri...]
    pallas_call x0 -> x1, Pallas kernels: none -> 2.69 us  [on_device(): pl.pallas_call(swap_kernel, out_shape=jax.ShapeDtypeStruct(cross.shape, j...]
    ppermute x1 -> x0, waiting for transfers between devices: 2.66 us -> none  [on_device(): other = lax.ppermute(cross, 'col', within)]
    unnamed x17 -> x19, local copies, waits for them, and re-layouts: 8.34 us -> 8.42 us
  transfers between devices with their start and end apart: 2 -> 1, of which waited for: 1 -> 0; matrix products, arithmetic and copies ran while one was open for 0% -> 0% of each run, Pallas kernels for 36% -> 39%
where the time goes in v4:
time: 85.8 us; the launch traced here: 85.4 us
  Pallas kernels  75.3 us (88%)
  local copies, waits for them, and re-layouts  8.63 us (10%)
    pallas_call x1, Pallas kernels, on_device(): pl.pallas_call(functools.partial(reduce_kernel, box_total, col_count, gro...  26.4 us
    pallas_call x1, Pallas kernels, on_device(): pl.pallas_call(solve_kernel, out_shape=jax.ShapeDtypeStruct((2, S, rest),...  18 us
    pallas_call x1, Pallas kernels, on_device(): pl.pallas_call(functools.partial(tile_kernel, box_count, box_total, entri...  11 us
    pallas_call x1, Pallas kernels, on_device(): pl.pallas_call(functools.partial(exchange_kernel, box_total, col_count, g...  10.3 us
    unnamed x19, local copies, waits for them, and re-layouts  8.42 us
    pallas_call x1, Pallas kernels, on_device(): pl.pallas_call(functools.partial(update_kernel, box_count, box_total, ent...  6.9 us
    pallas_call x1, Pallas kernels, on_device(): pl.pallas_call(swap_kernel, out_shape=jax.ShapeDtypeStruct(cross.shape, j...  2.69 us
  transfers between devices with their start and end apart: 1, of which 0 were waited for; matrix products, arithmetic and copies ran while one was open for 0% of the time, Pallas kernels for 39%

profile of v4, /device:TPU:0, one launch (start us, length us, event | category | flops | bytes accessed | tf_op | source)
XLA Modules:
  0.0 85.4 jit_solution(12375332939062738545)
XLA Ops:
  0.6 0.0 copy-start.6
  0.7 1.3 %copy.8.points_ref = f32[2,3,512]{2,1,0:T(4,128)} copy(f32[2,3,512]{2,0,1:T(2,128)} %param.6) | data formatting | bytes 24576 | tf_op args[0]
  2.0 0.1 pad_add_fusion.where_ref
  2.1 10.3 %shard_map.77 = (f32[3,2,3,512]{3,2,1,0:T(4,128)}, s32[3,2,512]{2,1,0:T(2,128)}, f32[2,3,256]{2,1,0:T(4,128)}, f32[4,2,2,64]{3,2,1,0:T(2,128)}) custom-call(f32[2,3,512]{2,1,0:T(4,128)} %copy.8.points_ref, s32[2,512]{1,0:T(2,128)} %order_ref.1, f32[3,256]{1,0:T(4,128)} %proxy_ref.1, f32[2,2,64]{2,1,0:T(2,128)} %pivot_ref.1), custom_call_target="tpu_custom_call" | custom-call | tf_op jit(solution)/shard_map/pallas_call | solution.py:416
  12.4 0.0 copy-start.1
  12.4 0.8 copy-done.1
  13.2 0.0 copy-start.2
  13.2 0.7 copy-done.2
  13.9 0.0 copy-start.4
  13.9 0.7 copy-done.4
  14.6 0.0 copy-start.5
  14.6 0.7 copy-done.5
  15.3 0.0 copy-start.7
  15.3 0.7 copy-done.7
  16.0 0.0 copy-start.3
  16.0 11.0 %shard_map.78 = (f32[2,256,512]{2,1,0:T(8,128)S(1)}, f32[4,2,256,512]{3,2,1,0:T(8,128)S(1)}) custom-call(s32[3]{0:T(128)S(1)} %pad_add_fusion.where_ref, s32[2,8]{1,0:T(2,128)S(1)} %copy-done.5, s32[2,8]{1,0:T(2,128)S(1)} %copy-done.7, f32[3,2,3,512]{3,2,1,0:T(4,128)S(1)} %copy-done.1, s32[3,2,512]{2,1,0:T(2,128)S(1)} %copy-done.2, f32[2,3,256]{2,1,0:T(4,128)S(1)} %copy-done.4), custom_call_target="tpu_custom_call" | custom-call | tf_op jit(solution)/shard_map/pallas_call | solution.py:433
  26.9 0.0 copy-start
  27.0 1.9 %copy-done = f32[4,2,256,512]{3,2,1,0:T(8,128)} copy-done((f32[4,2,256,512]{3,2,1,0:T(8,128)}, f32[4,2,256,512]{3,2,1,0:T(8,128)S(1)}, u32[]{:S(2)}) %copy-start) | copy-done | bytes 4194328
  28.9 2.7 %shard_map.79.other_ref = f32[2,256,512]{2,1,0:T(8,128)S(1)} custom-call(f32[2,256,512]{2,1,0:T(8,128)S(1)} %get-tuple-element.11.mine_ref), custom_call_target="tpu_custom_call" | custom-call | tf_op jit(solution)/shard_map/pallas_call | solution.py:451
  31.6 18.0 %shard_map.80.x_ref = f32[2,256,256]{2,1,0:T(8,128)S(1)} custom-call(f32[2,256,512]{2,1,0:T(8,128)S(1)} %get-tuple-element.11.mine_ref, f32[2,256,512]{2,1,0:T(8,128)S(1)} %shard_map.79.other_ref), custom_call_target="tpu_custom_call" | custom-call | tf_op jit(solution)/shard_map/pallas_call | solution.py:460
  49.6 0.2 dynamic-slice_bitcast_fusion
  49.8 0.6 collective-permute-start
  50.4 0.0 copy-done.6
  50.4 0.0 copy-done.3
  50.4 6.9 %shard_map.81 = f32[6,2,256,256]{3,2,1,0:T(8,128)S(1)} custom-call(s32[3]{0:T(128)S(1)} %pad_add_fusion.where_ref, s32[2,8]{1,0:T(2,128)S(1)} %copy-done.6, f32[4,2,256,512]{3,2,1,0:T(8,128)} %copy-done, f32[2,256,256]{2,1,0:T(8,128)S(1)} %shard_map.80.x_ref, f32[4,2,2,64]{3,2,1,0:T(2,128)S(1)} %copy-done.3), custom_call_target="tpu_custom_call" | custom-call | tf_op jit(solution)/shard_map/pallas_call | solution.py:479
  57.3 26.4 %shard_map.82 = f32[2,2,64,256]{3,2,1,0:T(8,128)S(1)} custom-call(f32[6,2,4,64,256]{4,3,2,1,0:T(8,128)S(1)} %bitcast.7), custom_call_target="tpu_custom_call" | custom-call | tf_op jit(solution)/shard_map/pallas_call | solution.py:489
  83.8 0.0 collective-permute-done
  83.8 0.9 %copy.9 = f32[2,2,256,64]{2,3,1,0:T(8,128)} copy(f32[2,2,256,64]{3,2,1,0:T(8,128)S(1)} %maximum_select_fusion) | data formatting | bytes 524288
  84.7 0.7 copy.11
  (1 shorter events, 0.0 us)
Async XLA Ops:
  0.6 49.8 %copy-start.6 = (s32[2,8]{1,0:T(2,128)S(1)}, s32[2,8]{1,0:T(2,128)}, u32[]{:S(2)}) copy-start(s32[2,8]{1,0:T(2,128)} %nb_ref.3) | copy-start | bytes 196
  12.4 0.8 copy-start.1
  13.2 0.7 copy-start.2
  13.9 0.7 copy-start.4
  14.6 0.7 copy-start.5
  15.3 0.7 copy-start.7
  16.0 34.5 %copy-start.3 = (f32[4,2,2,64]{3,2,1,0:T(2,128)S(1)}, f32[4,2,2,64]{3,2,1,0:T(2,128)}, u32[]{:S(2)}) copy-start(f32[4,2,2,64]{3,2,1,0:T(2,128)} %get-tuple-element.13.pivot_ref) | copy-start | bytes 12292
  26.9 2.0 %copy-start = (f32[4,2,256,512]{3,2,1,0:T(8,128)}, f32[4,2,256,512]{3,2,1,0:T(8,128)S(1)}, u32[]{:S(2)}) copy-start(f32[4,2,256,512]{3,2,1,0:T(8,128)S(1)} %get-tuple-element.12.kern_ref) | copy-start | bytes 12582916
  49.8 33.9 %collective-permute-start = (f32[2,256,64]{2,1,0:T(8,128)S(1)}, f32[2,256,64]{2,1,0:T(8,128)S(1)}, u32[]{:S(2)}, u32[]{:S(2)}) collective-permute-start(f32[2,256,64]{2,1,0:T(8,128)S(1)} %get-tuple-element.17), channel_id=1, source_target_pairs={{0,2},{1,3},{2,0},{3,1},{4,6},{5,7},{6,4},{7,5},{8,10},{9,11},{10,... | collective-permute-start | bytes 393224 | tf_op jit(solution)/shard_map/ppermute | solution.py:476

commit v5 on v4

--- a/solution.py
+++ b/solution.py
@@ -25,7 +25,7 @@
 
 
 def params(**more):
-    return pltpu.CompilerParams(vmem_limit_bytes=48 * 1024 * 1024, **more)
+    return pltpu.CompilerParams(vmem_limit_bytes=24 * 1024 * 1024, **more)
 
 
 def horner(coefficients, z):
@@ -425,7 +425,7 @@
         out_specs=(VMEM,) * 4,
         scratch_shapes=[pltpu.SemaphoreType.DMA((jobs,)), pltpu.SemaphoreType.DMA((jobs,)),
                         pltpu.SemaphoreType.DMA((4,))],
-        compiler_params=pltpu.CompilerParams(collective_id=0, has_side_effects=True),
+        compiler_params=params(collective_id=0, has_side_effects=True),
     )(box_points, point_order, proxy_directions, pivot_inverse)
 
     share = proxy_directions.shape[1]

time: 85.8 us -> 84.7 us (0.987)
  Pallas kernels: 75.3 us -> 72.8 us
  local copies, waits for them, and re-layouts: 8.63 us -> 10.1 us
    pallas_call x1, Pallas kernels: 6.9 us -> 5.24 us  [on_device(): pl.pallas_call(functools.partial(update_kernel, box_count, box_total, ent...]
    unnamed x19, local copies, waits for them, and re-layouts: 8.42 us -> 9.85 us
  transfers between devices with their start and end apart: 1 -> 1, of which waited for: 0 -> 0; matrix products, arithmetic and copies ran while one was open for 0% -> 0% of each run, Pallas kernels for 39% -> 38%
where the time goes in v5:
time: 84.7 us; the launch traced here: 84.3 us
  Pallas kernels  72.8 us (86%)
  local copies, waits for them, and re-layouts  10.1 us (12%)
    pallas_call x1, Pallas kernels, on_device(): pl.pallas_call(functools.partial(reduce_kernel, box_total, col_count, gro...  26.4 us
    pallas_call x1, Pallas kernels, on_device(): pl.pallas_call(solve_kernel, out_shape=jax.ShapeDtypeStruct((2, S, rest),...  18 us
    pallas_call x1, Pallas kernels, on_device(): pl.pallas_call(functools.partial(tile_kernel, box_count, box_total, entri...  11 us
    unnamed x19, local copies, waits for them, and re-layouts  9.85 us
    pallas_call x1, Pallas kernels, on_device(): pl.pallas_call(functools.partial(exchange_kernel, box_total, col_count, g...  9.48 us
    pallas_call x1, Pallas kernels, on_device(): pl.pallas_call(functools.partial(update_kernel, box_count, box_total, ent...  5.24 us
    pallas_call x1, Pallas kernels, on_device(): pl.pallas_call(swap_kernel, out_shape=jax.ShapeDtypeStruct(cross.shape, j...  2.69 us
  transfers between devices with their start and end apart: 1, of which 0 were waited for; matrix products, arithmetic and copies ran while one was open for 0% of the time, Pallas kernels for 38%

profile of v5, /device:TPU:0, one launch (start us, length us, event | category | flops | bytes accessed | tf_op | source)
XLA Modules:
  0.0 84.3 jit_solution(15790618578099494919)
XLA Ops:
  0.6 0.0 copy-start.3
  0.7 0.7 copy.8.points_ref
  1.4 0.1 pad_add_fusion.where_ref
  1.5 0.0 copy-start.4
  1.5 0.7 copy-done.4
  2.1 0.0 copy-start.5
  2.1 0.7 copy-done.5
  2.8 0.0 copy-start.6
  2.8 0.7 copy-done.6
  3.5 9.5 %shard_map.77 = (f32[3,2,3,512]{3,2,1,0:T(4,128)S(1)}, s32[3,2,512]{2,1,0:T(2,128)S(1)}, f32[2,3,256]{2,1,0:T(4,128)S(1)}, f32[4,2,2,64]{3,2,1,0:T(2,128)S(1)}) custom-call(f32[2,3,512]{2,1,0:T(4,128)S(1)} %copy.8.points_ref, s32[2,512]{1,0:T(2,128)S(1)} %copy-done.4, f32[3,256]{1,0:T(4,128)S(1)} %copy-done.5, f32[2,2,64]{2,1,0:T(2,128)S(1)} %copy-done.6), custom_call_target="tpu_custom_call" | custom-call | tf_op jit(solution)/shard_map/pallas_call | solution.py:416
  13.0 0.0 copy-start.2
  13.0 0.7 copy-done.2
  13.7 0.0 copy-start.7
  13.7 0.7 copy-done.7
  14.4 11.0 %shard_map.78 = (f32[2,256,512]{2,1,0:T(8,128)S(1)}, f32[4,2,256,512]{3,2,1,0:T(8,128)S(1)}) custom-call(s32[3]{0:T(128)S(1)} %pad_add_fusion.where_ref, s32[2,8]{1,0:T(2,128)S(1)} %copy-done.2, s32[2,8]{1,0:T(2,128)S(1)} %copy-done.7, f32[3,2,3,512]{3,2,1,0:T(4,128)S(1)} %get-tuple-element.8.points_ref, s32[3,2,512]{2,1,0:T(2,128)S(1)} %get-tuple-element.9.order_ref, ...), custom_call_target="tpu_custom_call" | custom-call | tf_op jit(solution)/shard_map/pallas_call | solution.py:433
  25.4 0.0 copy-start
  25.4 1.9 %copy-done = f32[4,2,256,512]{3,2,1,0:T(8,128)} copy-done((f32[4,2,256,512]{3,2,1,0:T(8,128)}, f32[4,2,256,512]{3,2,1,0:T(8,128)S(1)}, u32[]{:S(2)}) %copy-start) | copy-done | bytes 4194328
  27.3 2.7 %shard_map.79.other_ref = f32[2,256,512]{2,1,0:T(8,128)S(1)} custom-call(f32[2,256,512]{2,1,0:T(8,128)S(1)} %get-tuple-element.11.mine_ref), custom_call_target="tpu_custom_call" | custom-call | tf_op jit(solution)/shard_map/pallas_call | solution.py:451
  30.0 18.0 %shard_map.80.x_ref = f32[2,256,256]{2,1,0:T(8,128)S(1)} custom-call(f32[2,256,512]{2,1,0:T(8,128)S(1)} %get-tuple-element.11.mine_ref, f32[2,256,512]{2,1,0:T(8,128)S(1)} %shard_map.79.other_ref), custom_call_target="tpu_custom_call" | custom-call | tf_op jit(solution)/shard_map/pallas_call | solution.py:460
  48.0 0.2 dynamic-slice_bitcast_fusion
  48.2 0.6 collective-permute-start
  48.8 0.0 copy-done.3
  48.8 0.0 copy-start.1
  48.8 2.2 %copy-done.1 = f32[4,2,256,512]{3,2,1,0:T(8,128)S(1)} copy-done((f32[4,2,256,512]{3,2,1,0:T(8,128)S(1)}, f32[4,2,256,512]{3,2,1,0:T(8,128)}, u32[]{:S(2)}) %copy-start.1) | copy-done | bytes 4194328
  51.0 5.2 %shard_map.81 = f32[6,2,256,256]{3,2,1,0:T(8,128)S(1)} custom-call(s32[3]{0:T(128)S(1)} %pad_add_fusion.where_ref, s32[2,8]{1,0:T(2,128)S(1)} %copy-done.3, f32[4,2,256,512]{3,2,1,0:T(8,128)S(1)} %copy-done.1, f32[2,256,256]{2,1,0:T(8,128)S(1)} %shard_map.80.x_ref, f32[4,2,2,64]{3,2,1,0:T(2,128)S(1)} %get-tuple-element.13.pivot_ref), custom_call_target="tpu_custom_call" | custom-call | tf_op jit(solution)/shard_map/pallas_call | solution.py:479
  56.3 26.4 %shard_map.82 = f32[2,2,64,256]{3,2,1,0:T(8,128)S(1)} custom-call(f32[6,2,4,64,256]{4,3,2,1,0:T(8,128)S(1)} %bitcast.7), custom_call_target="tpu_custom_call" | custom-call | tf_op jit(solution)/shard_map/pallas_call | solution.py:489
  82.7 0.0 collective-permute-done
  82.7 0.9 %copy.9 = f32[2,2,256,64]{2,3,1,0:T(8,128)} copy(f32[2,2,256,64]{3,2,1,0:T(8,128)S(1)} %maximum_select_fusion) | data formatting | bytes 524288
  83.6 0.7 copy.11
  (1 shorter events, 0.0 us)
Async XLA Ops:
  0.6 48.2 %copy-start.3 = (s32[2,8]{1,0:T(2,128)S(1)}, s32[2,8]{1,0:T(2,128)}, u32[]{:S(2)}) copy-start(s32[2,8]{1,0:T(2,128)} %nb_ref.3) | copy-start | bytes 196
  1.5 0.7 copy-start.4
  2.1 0.7 copy-start.5
  2.8 0.7 copy-start.6
  13.0 0.7 copy-start.2
  13.7 0.7 copy-start.7
  25.4 2.0 %copy-start = (f32[4,2,256,512]{3,2,1,0:T(8,128)}, f32[4,2,256,512]{3,2,1,0:T(8,128)S(1)}, u32[]{:S(2)}) copy-start(f32[4,2,256,512]{3,2,1,0:T(8,128)S(1)} %get-tuple-element.12.kern_ref) | copy-start | bytes 12582916
  48.2 34.4 %collective-permute-start = (f32[2,256,64]{2,1,0:T(8,128)S(1)}, f32[2,256,64]{2,1,0:T(8,128)S(1)}, u32[]{:S(2)}, u32[]{:S(2)}) collective-permute-start(f32[2,256,64]{2,1,0:T(8,128)S(1)} %get-tuple-element.17), channel_id=1, source_target_pairs={{0,2},{1,3},{2,0},{3,1},{4,6},{5,7},{6,4},{7,5},{8,10},{9,11},{10,... | collective-permute-start | bytes 393224 | tf_op jit(solution)/shard_map/ppermute | solution.py:476
  48.8 2.2 %copy-start.1 = (f32[4,2,256,512]{3,2,1,0:T(8,128)S(1)}, f32[4,2,256,512]{3,2,1,0:T(8,128)}, u32[]{:S(2)}) copy-start(f32[4,2,256,512]{3,2,1,0:T(8,128)} %copy-done) | copy-start | bytes 12582916
